TPU v7x, 256 devices: a whole 4x4x8 slice. The times are simulated.
256 devices in a mesh: panel: 8 (over x, y_hi), leaf: 32 (over y_lo, z, core).
Axes of the slice: x: 4, y: 4 (y_hi: 2, y_lo: 2; y = y_hi * 2 + y_lo), z: 8, core: 2. Of those that a mesh axis runs over, the one named last changes fastest.
Arguments:
- excitation: bfloat16 [2, 128, 786432], P(None, None, ('panel', 'leaf')), may hold values from -6 to 6
- point_order: int32 [256, 3072], P(('panel', 'leaf')), may hold values from 0 to 3071, each once within a row
- projection: bfloat16 [2, 256, 786432], P(None, None, ('panel', 'leaf')), may hold values from -0.078125 to 0.078125
- transfer: bfloat16 [5, 2, 65536, 512], P(None, None, ('panel', 'leaf')), may hold values from -0.1875 to 0.1875
- expansion: bfloat16 [2, 256, 786432], P(None, None, ('panel', 'leaf')), may hold values from -0.09375 to 0.09375
Outputs:
- response: bfloat16 [2, 128, 786432], P(None, None, ('panel', 'leaf'))
Inputs may be any that keep to these rules, and one draw needn't show every extreme that they name: Each row of point_order holds every number of 0 to 3071 once.
All inputs are finite; a program needn't handle non-finite values.
Results may differ from a plain program's by a relative error of at most 0.018.
Values may be sent and summed in bfloat16 or wider, within the bound.
No kernel may reach another device: no remote copies, remote signals or barrier semaphores. Data moves between devices by JAX's collectives and lax.ppermute only.
A program may use at most 64 MiB of HBM per device.

v0:
```python
import jax
import jax.numpy as jnp
from jax import lax
from jax.sharding import PartitionSpec as P


def partner_2(block, axis, stride):
    count = lax.axis_size(axis)
    route = []
    for low in range(count):
        high = low | 1 << stride
        if high != low and high < count:
            route += [(low, high), (high, low)]
    return lax.ppermute(block, axis, route)


def copy_for_each(x, axis):
    count = lax.axis_size(axis)
    return lax.all_to_all(jnp.broadcast_to(x[None], (count, *x.shape)), axis, 0, 0, tiled=True)


def taken_together(x, axis):
    return copy_for_each(x, axis).astype(jnp.float32).sum(axis=0)


def complex_dot(first_matrix, second_matrix, first_dim, second_dim):
    contract = (((first_dim,), (second_dim,)), ((), ()))

    def real_dot(first_part, second_part):
        return lax.dot_general(
            first_part, second_part, contract, preferred_element_type=jnp.float32
        )

    real_part = real_dot(first_matrix[0], second_matrix[0]) - real_dot(
        first_matrix[1], second_matrix[1]
    )
    imag_part = real_dot(first_matrix[0], second_matrix[1]) + real_dot(
        first_matrix[1], second_matrix[0]
    )
    return jnp.stack((real_part, imag_part))


def per_device(excitation, point_order, projection, transfer, expansion):
    gathered = jnp.take(excitation, point_order[0], axis=2)
    coefficients = complex_dot(projection, gathered, 1, 1).astype(jnp.bfloat16)
    position = lax.axis_index("leaf")
    rank_width = coefficients.shape[1]
    for level in range(lax.axis_size("leaf").bit_length() - 1):
        partner = partner_2(coefficients, "leaf", level)
        upper_bit = position >> level & 1 == 1
        matrix = transfer[level]
        first_block = matrix[:, :, :rank_width]
        second_block = matrix[:, :, rank_width:]
        own_matrix = jnp.where(upper_bit, second_block, first_block)
        other_matrix = jnp.where(upper_bit, first_block, second_block)
        own_term = complex_dot(own_matrix, coefficients, 1, 0)
        partner_term = complex_dot(other_matrix, partner, 1, 0)
        coefficients = (own_term + partner_term).astype(jnp.bfloat16)
    summed = taken_together(coefficients.astype(jnp.float32).astype(jnp.bfloat16), "panel").astype(
        jnp.float32
    )
    summed = summed.astype(jnp.bfloat16)
    result = complex_dot(summed, expansion, 0, 0)
    return result.astype(jnp.bfloat16)


def solution(mesh):
    in_specs = (
        P(None, None, ("panel", "leaf")),
        P(("panel", "leaf"), None),
        P(None, None, ("panel", "leaf")),
        P(None, None, ("panel", "leaf"), None),
        P(None, None, ("panel", "leaf")),
    )
    out_specs = P(None, None, ("panel", "leaf"))
    return jax.shard_map(
        per_device, mesh=mesh, in_specs=in_specs, out_specs=out_specs, check_vma=False
    )
```

profile of v0, /device:TPU:96, one launch (start us, length us, event | category | flops | bytes accessed | tf_op | source)
XLA Modules:
  0.0 100.7 jit_solution(925574069708296753)
XLA Ops:
  0.0 3.6 %copy.10 = bf16[2,128,3072]{1,0,2:T(2,128)(2,1)S(1)} copy(bf16[2,128,3072]{2,1,0:T(8,128)(2,1)} %param.5) | data formatting | bytes 3145728 | tf_op args[0]
  3.7 10.4 %gather_fusion = bf16[3072,2,128]{2,1,0:T(2,128)(2,1)S(1)} fusion(bf16[2,128,3072]{1,0,2:T(2,128)(2,1)S(1)} %copy.10, s32[3072]{0:T(1024)S(1)} %broadcast_clamp_fusion), kind=kCustom, calls=%fused_computation | custom fusion | bytes 3158016 | tf_op jit(solution)/shard_map/jit(_take)/gather | solution.py:44
  14.1 11.1 %fusion.18 = bf16[2,128,3072]{1,0,2:T(2,128)(2,1)S(1)} fusion(bf16[3072,2,128]{2,1,0:T(2,128)(2,1)S(1)} %gather_fusion, pred[3072]{0:T(1024)(128)(4,1)S(1)} %compare_and_fusion), kind=kLoop, calls=%fused_computation.23 | loop fusion | flops 786432 | bytes 3148800 | tf_op jit(solution)/shard_map/jit(_take)/select_n | solution.py:44
  25.2 2.2 %fusion.88 = (bf16[1,128,3072]{1,0,2:T(2,128)(2,1)S(1)}, bf16[1,128,3072]{1,0,2:T(2,128)(2,1)S(1)}) fusion(bf16[2,128,3072]{1,0,2:T(2,128)(2,1)S(1)} %fusion.18), kind=kLoop, calls=%fused_computation.170 | loop fusion | bytes 3145728 | tf_op jit(solution)/shard_map/slice | solution.py:35
  27.5 2.9 %copy.12 = bf16[1,128,3072]{2,1,0:T(8,128)(2,1)} copy(bf16[1,128,3072]{1,0,2:T(2,128)(2,1)S(1)} %get-tuple-element.10) | data formatting | bytes 1572864 | tf_op jit(solution)/shard_map/slice | solution.py:35
  30.4 1.6 %copy.11 = bf16[1,128,3072]{2,1,0:T(8,128)(2,1)S(1)} copy(bf16[1,128,3072]{1,0,2:T(2,128)(2,1)S(1)} %get-tuple-element.11) | data formatting | bytes 1572864 | tf_op jit(solution)/shard_map/slice | solution.py:34
  32.0 2.2 %fusion.12 = f32[128,256]{1,0:T(8,128)S(1)} fusion(bf16[2,256,3072]{2,1,0:T(8,128)(2,1)} %param.7, bf16[1,128,3072]{2,1,0:T(8,128)(2,1)S(1)} %copy-done.2), kind=kOutput, calls=%fused_computation.17 | convolution fusion | flops 201326592 | bytes 2490368 | tf_op jit(solution)/shard_map/dot_general | solution.py:30
  34.2 2.1 %fusion.10 = f32[128,256]{1,0:T(8,128)S(1)} fusion(bf16[2,256,3072]{2,1,0:T(8,128)(2,1)} %param.7, bf16[1,128,3072]{2,1,0:T(8,128)(2,1)S(1)} %copy.11), kind=kOutput, calls=%fused_computation.15 | convolution fusion | flops 201326592 | bytes 2490368 | tf_op jit(solution)/shard_map/dot_general | solution.py:30
  36.3 0.7 fusion.56
  37.0 0.7 fusion.53
  37.8 0.9 copy-done.1
  38.7 0.3 slice_bitcast_fusion
  39.6 0.2 fusion.52
  39.8 0.2 fusion.51
  40.2 0.2 fusion.78
  40.4 0.2 fusion.50
  40.6 0.2 fusion.49
  40.8 0.2 collective-permute-start.1
  41.7 4.4 %collective-permute-done.1 = bf16[2,256,128]{2,1,0:T(8,128)(2,1)S(1)} collective-permute-done((bf16[2,256,128]{2,1,0:T(8,128)(2,1)S(1)}, bf16[2,256,128]{2,1,0:T(8,128)(2,1)S(1)}, u32[]{:S(2)}, u32[]{:S(2)}) %collective-permute-start.1) | collective-permute-done | bytes 131104 | tf_op jit(solution)/shard_map/ppermute | solution.py:14
  47.7 7.3 %collective-permute-done.2 = bf16[2,256,128]{2,1,0:T(8,128)(2,1)S(1)} collective-permute-done((bf16[2,256,128]{2,1,0:T(8,128)(2,1)S(1)}, bf16[2,256,128]{2,1,0:T(8,128)(2,1)S(1)}, u32[]{:S(2)}, u32[]{:S(2)}) %collective-permute-start.2) | collective-permute-done | bytes 131104 | tf_op jit(solution)/shard_map/ppermute | solution.py:14
  55.7 4.7 %collective-permute-start.3 = (bf16[2,256,128]{2,1,0:T(8,128)(2,1)S(1)}, bf16[2,256,128]{2,1,0:T(8,128)(2,1)S(1)}, u32[]{:S(2)}, u32[]{:S(2)}) collective-permute-start(bf16[2,256,128]{2,1,0:T(8,128)(2,1)S(1)} %fusion.65), channel_id=1, source_target_pairs={{0,8},{8,0},{1,9},{9,1},{2,10},{10,2},{3,11},{11,3},{4,12},{12,4},... | collective-permute-start | bytes 393224 | tf_op jit(solution)/shard_map/ppermute | solution.py:14
  61.1 6.5 %collective-permute-done.3 = bf16[2,256,128]{2,1,0:T(8,128)(2,1)S(1)} collective-permute-done((bf16[2,256,128]{2,1,0:T(8,128)(2,1)S(1)}, bf16[2,256,128]{2,1,0:T(8,128)(2,1)S(1)}, u32[]{:S(2)}, u32[]{:S(2)}) %collective-permute-start.3) | collective-permute-done | bytes 131104 | tf_op jit(solution)/shard_map/ppermute | solution.py:14
  68.3 1.7 %collective-permute-start.4 = (bf16[2,256,128]{2,1,0:T(8,128)(2,1)S(1)}, bf16[2,256,128]{2,1,0:T(8,128)(2,1)S(1)}, u32[]{:S(2)}, u32[]{:S(2)}) collective-permute-start(bf16[2,256,128]{2,1,0:T(8,128)(2,1)S(1)} %fusion.66), channel_id=1, source_target_pairs={{0,16},{16,0},{1,17},{17,1},{2,18},{18,2},{3,19},{19,3},{4,20},{20... | collective-permute-start | bytes 393224 | tf_op jit(solution)/shard_map/ppermute | solution.py:14
  70.7 2.7 %collective-permute-done.4 = bf16[2,256,128]{2,1,0:T(8,128)(2,1)S(1)} collective-permute-done((bf16[2,256,128]{2,1,0:T(8,128)(2,1)S(1)}, bf16[2,256,128]{2,1,0:T(8,128)(2,1)S(1)}, u32[]{:S(2)}, u32[]{:S(2)}) %collective-permute-start.4) | collective-permute-done | bytes 131104 | tf_op jit(solution)/shard_map/ppermute | solution.py:14
  74.1 0.2 broadcast_in_dim.18
  74.4 22.0 %all_to_all.5 = bf16[8,2,256,128]{3,2,1,0:T(8,128)(2,1)} all-to-all(bf16[8,2,256,128]{3,2,1,0:T(8,128)(2,1)S(1)} %broadcast_in_dim.18), channel_id=1, replica_groups=mesh['panel'=8,'leaf'=32] {'panel'}, dimensions={0} | all-to-all | bytes 2097152 | tf_op jit(solution)/shard_map/all_to_all | solution.py:19
  96.3 1.4 %reduce_sum.12 = bf16[2,256,128]{2,1,0:T(8,128)(2,1)S(1)} reduce(bf16[8,2,256,128]{3,2,1,0:T(8,128)(2,1)} %all_to_all.5, bf16[]{:T(256)} %constant.31.clone.1), dimensions={0}, to_apply=%region_0.1 | reduce | flops 458752 | bytes 1179650 | tf_op jit(solution)/shard_map/reduce_sum | solution.py:23
  97.7 0.4 fusion.8
  98.1 0.4 fusion.4
  98.5 0.4 fusion.3
  99.0 0.4 fusion.2
  99.4 1.3 %pad_maximum_fusion = bf16[2,128,3072]{2,1,0:T(8,128)(2,1)} fusion(bf16[1,128,3072]{2,1,0:T(8,128)(2,1)S(1)} %fusion.2, bf16[1,128,3072]{2,1,0:T(8,128)(2,1)S(1)} %fusion.3), kind=kLoop, calls=%fused_computation.8 | loop fusion | flops 786432 | bytes 3145728 | tf_op jit(solution)/shard_map/stack | solution.py:40
  (61 shorter events, 6.5 us)
Async XLA Ops:
  0.0 3.6 %copy-start.3 = (s32[1,3072]{1,0:T(1,128)S(1)}, s32[1,3072]{1,0:T(1,128)}, u32[]{:S(2)}) copy-start(s32[1,3072]{1,0:T(1,128)} %param.6) | copy-start | bytes 36868
  30.4 1.6 %copy-start.2 = (bf16[1,128,3072]{2,1,0:T(8,128)(2,1)S(1)}, bf16[1,128,3072]{2,1,0:T(8,128)(2,1)}, u32[]{:S(2)}) copy-start(bf16[1,128,3072]{2,1,0:T(8,128)(2,1)} %copy.12) | copy-start | bytes 2359300
  32.0 4.3 %copy-start.4 = (bf16[2,256,3072]{2,1,0:T(8,128)(2,1)S(1)}, bf16[2,256,3072]{2,1,0:T(8,128)(2,1)}, u32[]{:S(2)}) copy-start(bf16[2,256,3072]{2,1,0:T(8,128)(2,1)} %param.7) | copy-start | bytes 9437188
  37.0 1.7 %copy-start.1 = (bf16[5,2,256,512]{3,2,1,0:T(8,128)(2,1)S(1)}, bf16[5,2,256,512]{3,2,1,0:T(8,128)(2,1)}, u32[]{:S(2)}) copy-start(bf16[5,2,256,512]{3,2,1,0:T(8,128)(2,1)} %param.8) | copy-start | bytes 7864324
  37.7 2.3 %collective-permute-start = (bf16[2,256,128]{1,2,0:T(8,128)(2,1)S(1)}, bf16[2,256,128]{1,2,0:T(8,128)(2,1)S(1)}, u32[]{:S(2)}, u32[]{:S(2)}) collective-permute-start(bf16[2,256,128]{1,2,0:T(8,128)(2,1)S(1)} %pad_maximum_fusion.1), channel_id=1, source_target_pairs={{0,1},{1,0},{2,3},{3,2},{4,5},{5,4},{6,7},{7,6},{8,9},{9,8},{10,11... | collective-permute-start | bytes 393224 | tf_op jit(solution)/shard_map/ppermute | solution.py:14
  40.8 5.3 %collective-permute-start.1 = (bf16[2,256,128]{2,1,0:T(8,128)(2,1)S(1)}, bf16[2,256,128]{2,1,0:T(8,128)(2,1)S(1)}, u32[]{:S(2)}, u32[]{:S(2)}) collective-permute-start(bf16[2,256,128]{2,1,0:T(8,128)(2,1)S(1)} %fusion.63), channel_id=1, source_target_pairs={{0,2},{2,0},{1,3},{3,1},{4,6},{6,4},{5,7},{7,5},{8,10},{10,8},{9,1... | collective-permute-start | bytes 393224 | tf_op jit(solution)/shard_map/ppermute | solution.py:14
  46.9 8.1 %collective-permute-start.2 = (bf16[2,256,128]{2,1,0:T(8,128)(2,1)S(1)}, bf16[2,256,128]{2,1,0:T(8,128)(2,1)S(1)}, u32[]{:S(2)}, u32[]{:S(2)}) collective-permute-start(bf16[2,256,128]{2,1,0:T(8,128)(2,1)S(1)} %fusion.64), channel_id=1, source_target_pairs={{0,4},{4,0},{1,5},{5,1},{2,6},{6,2},{3,7},{7,3},{8,12},{12,8},{9,1... | collective-permute-start | bytes 393224 | tf_op jit(solution)/shard_map/ppermute | solution.py:14
  55.7 11.9 %collective-permute-start.3 = (bf16[2,256,128]{2,1,0:T(8,128)(2,1)S(1)}, bf16[2,256,128]{2,1,0:T(8,128)(2,1)S(1)}, u32[]{:S(2)}, u32[]{:S(2)}) collective-permute-start(bf16[2,256,128]{2,1,0:T(8,128)(2,1)S(1)} %fusion.65), channel_id=1, source_target_pairs={{0,8},{8,0},{1,9},{9,1},{2,10},{10,2},{3,11},{11,3},{4,12},{12,4},... | collective-permute-start | bytes 393224 | tf_op jit(solution)/shard_map/ppermute | solution.py:14
  68.3 5.1 %collective-permute-start.4 = (bf16[2,256,128]{2,1,0:T(8,128)(2,1)S(1)}, bf16[2,256,128]{2,1,0:T(8,128)(2,1)S(1)}, u32[]{:S(2)}, u32[]{:S(2)}) collective-permute-start(bf16[2,256,128]{2,1,0:T(8,128)(2,1)S(1)} %fusion.66), channel_id=1, source_target_pairs={{0,16},{16,0},{1,17},{17,1},{2,18},{18,2},{3,19},{19,3},{4,20},{20... | collective-permute-start | bytes 393224 | tf_op jit(solution)/shard_map/ppermute | solution.py:14
  74.4 23.4 %copy-start = (bf16[2,256,3072]{2,1,0:T(8,128)(2,1)S(1)}, bf16[2,256,3072]{2,1,0:T(8,128)(2,1)}, u32[]{:S(2)}) copy-start(bf16[2,256,3072]{2,1,0:T(8,128)(2,1)} %param.9) | copy-start | bytes 9437188
where the time goes:
time: 101 us
  local copies, waits for them, and re-layouts  22.2 us (22%)
  blocking collectives  22 us (22%)
  waiting for transfers between devices  20.9 us (21%)
  other arithmetic  14.2 us (14%)
  matrix products  14.1 us (14%)
  starting transfers between devices  6.73 us (7%)
    all_to_all x1, blocking collectives, copy_for_each(): lax.all_to_all(jnp.broadcast_to(x[None], (count, *x.shape)), axis, 0, 0,...  22 us
    ppermute x5, waiting for transfers between devices, partner_2(): return lax.ppermute(block, axis, route)  20.9 us
    dot_general x48, matrix products, real_dot(): lax.dot_general(first_part, second_part, contract, preferred_element_type...  14.1 us
    select_n x2, other arithmetic, per_device(): gathered = jnp.take(excitation, point_order[0], axis=2)  11.1 us
    gather x1, local copies, waits for them, and re-layouts, per_device(): gathered = jnp.take(excitation, point_order[0], axis=2)  10.4 us
    ppermute x5, starting transfers between devices, partner_2(): return lax.ppermute(block, axis, route)  6.73 us
    slice x2, local copies, waits for them, and re-layouts, complex_dot(): second_matrix[1]  5.11 us
    unnamed x11, local copies, waits for them, and re-layouts  4.56 us
  transfers between devices with their start and end apart: 5, of which 4 were waited for; matrix products, arithmetic and copies ran while one was open for 4% of the time, Pallas kernels for 0%

commit v1 on v0

--- a/solution.py
+++ b/solution.py
@@ -1,6 +1,10 @@
+import functools
+
 import jax
 import jax.numpy as jnp
 from jax import lax
+from jax.experimental import pallas as pl
+from jax.experimental.pallas import tpu as pltpu
 from jax.sharding import PartitionSpec as P
 
 
@@ -40,9 +44,56 @@
     return jnp.stack((real_part, imag_part))
 
 
+def leaf_kernel(order_ref, source_ref, basis_ref, out_ref, total_ref):
+    _, width, points = source_ref.shape
+    rank, chunk = basis_ref.shape[1:]
+    step = pl.program_id(0)
+    source = source_ref[...].reshape(2 * width, points)
+    point = lax.broadcasted_iota(jnp.int16, (points, chunk), 0)
+    chosen = jnp.where(
+        point == order_ref[...].astype(jnp.int16), jnp.bfloat16(1), jnp.bfloat16(0)
+    )
+    ordered = jnp.dot(source, chosen, preferred_element_type=jnp.float32).astype(jnp.bfloat16)
+    basis = basis_ref[...].reshape(2 * rank, chunk)
+    product = lax.dot_general(
+        basis, ordered, (((1,), (1,)), ((), ())), preferred_element_type=jnp.float32
+    )
+
+    @pl.when(step == 0)
+    def _():
+        total_ref[...] = product
+
+    @pl.when(step > 0)
+    def _():
+        total_ref[...] += product
+
+    @pl.when(step == pl.num_programs(0) - 1)
+    def _():
+        total = total_ref[...]
+        out_ref[0] = (total[:rank, :width] - total[rank:, width:]).astype(jnp.bfloat16)
+        out_ref[1] = (total[:rank, width:] + total[rank:, :width]).astype(jnp.bfloat16)
+
+
+def leaf_coefficients(excitation, point_order, projection, chunk=512):
+    _, width, points = excitation.shape
+    rank = projection.shape[1]
+    return pl.pallas_call(
+        leaf_kernel,
+        grid=(points // chunk,),
+        in_specs=[
+            pl.BlockSpec((1, chunk), lambda j: (0, j)),
+            pl.BlockSpec((2, width, points), lambda j: (0, 0, 0)),
+            pl.BlockSpec((2, rank, chunk), lambda j: (0, 0, j)),
+        ],
+        out_specs=pl.BlockSpec((2, rank, width), lambda j: (0, 0, 0)),
+        out_shape=jax.ShapeDtypeStruct((2, rank, width), jnp.bfloat16),
+        scratch_shapes=[pltpu.VMEM((2 * rank, 2 * width), jnp.float32)],
+        name="leaf",
+    )(point_order, excitation, projection)
+
+
 def per_device(excitation, point_order, projection, transfer, expansion):
-    gathered = jnp.take(excitation, point_order[0], axis=2)
-    coefficients = complex_dot(projection, gathered, 1, 1).astype(jnp.bfloat16)
+    coefficients = leaf_coefficients(excitation, point_order, projection)
     position = lax.axis_index("leaf")
     rank_width = coefficients.shape[1]
     for level in range(lax.axis_size("leaf").bit_length() - 1):
@@ -56,10 +107,7 @@
         own_term = complex_dot(own_matrix, coefficients, 1, 0)
         partner_term = complex_dot(other_matrix, partner, 1, 0)
         coefficients = (own_term + partner_term).astype(jnp.bfloat16)
-    summed = taken_together(coefficients.astype(jnp.float32).astype(jnp.bfloat16), "panel").astype(
-        jnp.float32
-    )
-    summed = summed.astype(jnp.bfloat16)
+    summed = taken_together(coefficients, "panel").astype(jnp.bfloat16)
     result = complex_dot(summed, expansion, 0, 0)
     return result.astype(jnp.bfloat16)
 

time: 101 us -> 77.1 us (0.76)
  local copies, waits for them, and re-layouts: 22.2 us -> 2.24 us
  Pallas kernels: 0 us -> 10.3 us
  other arithmetic: 14.2 us -> 4.13 us
  matrix products: 14.1 us -> 8.43 us
  waiting for transfers between devices: 20.9 us -> 22.5 us
    select_n x2 -> x0, other arithmetic: 11.1 us -> none  [per_device(): gathered = jnp.take(excitation, point_order[0], axis=2)]
    gather x1 -> x0, local copies, waits for them, and re-layouts: 10.4 us -> none  [per_device(): gathered = jnp.take(excitation, point_order[0], axis=2)]
    pallas_call x0 -> x1, Pallas kernels: none -> 10.3 us  [leaf_coefficients(): pl.pallas_call(leaf_kernel, grid=(points // chunk,), in_specs=[pl.BlockSp...]
    slice x3 -> x0, local copies, waits for them, and re-layouts: 6.72 us -> none  [the longest x2 5.11 us: complex_dot(): second_matrix[1]]
    dot_general x48 -> x44, matrix products: 14.1 us -> 8.43 us  [real_dot(): lax.dot_general(first_part, second_part, contract, preferred_element_type...]
    unnamed x11 -> x12, local copies, waits for them, and re-layouts: 4.56 us -> 0.61 us
    ppermute x5, waiting for transfers between devices: 20.9 us -> 22.5 us  [partner_2(): return lax.ppermute(block, axis, route)]
    squeeze x1, local copies, waits for them, and re-layouts: 0.28 us -> 1.43 us  [per_device(): matrix = transfer[level]]
  transfers between devices with their start and end apart: 5 -> 5, of which waited for: 4 -> 4; matrix products, arithmetic and copies ran while one was open for 4% -> 8% of each run, Pallas kernels for 0% -> 0%
where the time goes in v1:
time: 77.1 us; the launch traced here: 77 us
  waiting for transfers between devices  22.5 us (29%)
  blocking collectives  22.2 us (29%)
  Pallas kernels  10.3 us (13%)
  matrix products  8.43 us (11%)
  starting transfers between devices  6.64 us (9%)
  other arithmetic  4.13 us (5%)
  local copies, waits for them, and re-layouts  2.24 us (3%)
    ppermute x5, waiting for transfers between devices, partner_2(): return lax.ppermute(block, axis, route)  22.5 us
    all_to_all x1, blocking collectives, copy_for_each(): lax.all_to_all(jnp.broadcast_to(x[None], (count, *x.shape)), axis, 0, 0,...  22.2 us
    pallas_call x1, Pallas kernels, leaf_coefficients(): pl.pallas_call(leaf_kernel, grid=(points // chunk,), in_specs=[pl.BlockSp...  10.3 us
    dot_general x44, matrix products, real_dot(): lax.dot_general(first_part, second_part, contract, preferred_element_type...  8.43 us
    ppermute x5, starting transfers between devices, partner_2(): return lax.ppermute(block, axis, route)  6.64 us
  transfers between devices with their start and end apart: 5, of which 4 were waited for; matrix products, arithmetic and copies ran while one was open for 8% of the time, Pallas kernels for 0%

profile of v1, /device:TPU:96, one launch (start us, length us, event | category | flops | bytes accessed | tf_op | source)
XLA Modules:
  0.0 77.0 jit_solution(3255163225726002461)
XLA Ops:
  0.0 10.3 %leaf.1 = bf16[2,256,128]{2,1,0:T(8,128)(2,1)} custom-call(s32[1,3072]{1,0:T(1,128)} %order_ref.1, bf16[2,128,3072]{2,1,0:T(8,128)(2,1)} %source_ref.1, bf16[2,256,3072]{2,1,0:T(8,128)(2,1)} %basis_ref.1), custom_call_target="tpu_custom_call" | custom-call | tf_op jit(solution)/shard_map/leaf/pallas_call | solution.py:80
  10.3 1.4 %slice_bitcast_fusion = (bf16[2,256,512]{2,1,0:T(8,128)(2,1)}, bf16[2,256,512]{2,1,0:T(8,128)(2,1)}, bf16[2,256,512]{2,1,0:T(8,128)(2,1)}, bf16[2,256,512]{2,1,0:T(8,128)(2,1)S(1)}, bf16[2,256,512]{2,1,0:T(8,128)(2,1)}) fusion(bf16[5,2,256,512]{3,2,1,0:T(8,128)(2,1)S(1)} %copy-done.1), kind=kLoop, calls=%fused_computation.57 | loop fusion | bytes 5242880 | tf_op jit(solution)/shard_map/squeeze | solution.py:102
  11.8 1.2 %broadcast_select_fusion = (bf16[2,256,256]{2,1,0:T(8,128)(2,1)S(1)}, bf16[2,256,256]{2,1,0:T(8,128)(2,1)S(1)}) fusion(pred[]{:T(512)S(6)} %eq.19, bf16[2,256,512]{2,1,0:T(8,128)(2,1)} %get-tuple-element.5), kind=kLoop, calls=%fused_computation.72 | loop fusion | flops 262144 | bytes 1048577 | tf_op jit(solution)/shard_map/jit(_where)/select_n | solution.py:106
  13.4 0.6 copy-done.2
  14.1 0.2 fusion.33
  14.3 0.2 fusion.32
  14.8 0.2 fusion.31
  15.0 0.2 fusion.30
  15.2 0.2 collective-permute-start.1
  15.8 0.2 fusion.29
  16.1 5.1 %collective-permute-done.1 = bf16[2,256,128]{2,1,0:T(8,128)(2,1)S(1)} collective-permute-done((bf16[2,256,128]{2,1,0:T(8,128)(2,1)S(1)}, bf16[2,256,128]{2,1,0:T(8,128)(2,1)S(1)}, u32[]{:S(2)}, u32[]{:S(2)}) %collective-permute-start.1) | collective-permute-done | bytes 131104 | tf_op jit(solution)/shard_map/ppermute | solution.py:18
  21.5 0.2 fusion.27
  21.7 0.2 fusion.26
  22.4 0.2 fusion.25
  22.7 7.9 %collective-permute-done.2 = bf16[2,256,128]{2,1,0:T(8,128)(2,1)S(1)} collective-permute-done((bf16[2,256,128]{2,1,0:T(8,128)(2,1)S(1)}, bf16[2,256,128]{2,1,0:T(8,128)(2,1)S(1)}, u32[]{:S(2)}, u32[]{:S(2)}) %collective-permute-start.2) | collective-permute-done | bytes 131104 | tf_op jit(solution)/shard_map/ppermute | solution.py:18
  31.2 0.2 fusion.22
  31.4 4.7 %collective-permute-start.3 = (bf16[2,256,128]{2,1,0:T(8,128)(2,1)S(1)}, bf16[2,256,128]{2,1,0:T(8,128)(2,1)S(1)}, u32[]{:S(2)}, u32[]{:S(2)}) collective-permute-start(bf16[2,256,128]{2,1,0:T(8,128)(2,1)S(1)} %fusion.36), channel_id=1, source_target_pairs={{0,8},{8,0},{1,9},{9,1},{2,10},{10,2},{3,11},{11,3},{4,12},{12,4},... | collective-permute-start | bytes 393224 | tf_op jit(solution)/shard_map/ppermute | solution.py:18
  36.8 6.8 %collective-permute-done.3 = bf16[2,256,128]{2,1,0:T(8,128)(2,1)S(1)} collective-permute-done((bf16[2,256,128]{2,1,0:T(8,128)(2,1)S(1)}, bf16[2,256,128]{2,1,0:T(8,128)(2,1)S(1)}, u32[]{:S(2)}, u32[]{:S(2)}) %collective-permute-start.3) | collective-permute-done | bytes 131104 | tf_op jit(solution)/shard_map/ppermute | solution.py:18
  44.1 0.2 fusion.18
  44.4 1.7 %collective-permute-start.4 = (bf16[2,256,128]{2,1,0:T(8,128)(2,1)S(1)}, bf16[2,256,128]{2,1,0:T(8,128)(2,1)S(1)}, u32[]{:S(2)}, u32[]{:S(2)}) collective-permute-start(bf16[2,256,128]{2,1,0:T(8,128)(2,1)S(1)} %fusion.37), channel_id=1, source_target_pairs={{0,16},{16,0},{1,17},{17,1},{2,18},{18,2},{3,19},{19,3},{4,20},{20... | collective-permute-start | bytes 393224 | tf_op jit(solution)/shard_map/ppermute | solution.py:18
  46.4 0.2 fusion.17
  46.6 0.2 fusion.16
  46.7 2.7 %collective-permute-done.4 = bf16[2,256,128]{2,1,0:T(8,128)(2,1)S(1)} collective-permute-done((bf16[2,256,128]{2,1,0:T(8,128)(2,1)S(1)}, bf16[2,256,128]{2,1,0:T(8,128)(2,1)S(1)}, u32[]{:S(2)}, u32[]{:S(2)}) %collective-permute-start.4) | collective-permute-done | bytes 131104 | tf_op jit(solution)/shard_map/ppermute | solution.py:18
  49.9 0.2 fusion.14
  50.2 0.2 broadcast_in_dim.2
  50.4 22.2 %all_to_all.5 = bf16[8,2,256,128]{3,2,1,0:T(8,128)(2,1)} all-to-all(bf16[8,2,256,128]{3,2,1,0:T(8,128)(2,1)S(1)} %broadcast_in_dim.2), channel_id=1, replica_groups=mesh['panel'=8,'leaf'=32] {'panel'}, dimensions={0} | all-to-all | bytes 2097152 | tf_op jit(solution)/shard_map/all_to_all | solution.py:23
  72.6 1.4 %reduce_sum.12 = bf16[2,256,128]{2,1,0:T(8,128)(2,1)S(1)} reduce(bf16[8,2,256,128]{3,2,1,0:T(8,128)(2,1)} %all_to_all.5, bf16[]{:T(256)} %constant.16.clone.1), dimensions={0}, to_apply=%region_0.1 | reduce | flops 458752 | bytes 1179650 | tf_op jit(solution)/shard_map/reduce_sum | solution.py:27
  74.0 0.4 fusion.8
  74.4 0.4 fusion.4
  74.8 0.4 fusion.3
  75.2 0.4 fusion.2
  75.7 1.3 %pad_maximum_fusion = bf16[2,128,3072]{2,1,0:T(8,128)(2,1)} fusion(bf16[1,128,3072]{2,1,0:T(8,128)(2,1)S(1)} %fusion.2, bf16[1,128,3072]{2,1,0:T(8,128)(2,1)S(1)} %fusion.3), kind=kLoop, calls=%fused_computation.6 | loop fusion | flops 786432 | bytes 3145728 | tf_op jit(solution)/shard_map/stack | solution.py:44
  (50 shorter events, 5.0 us)
Async XLA Ops:
  0.0 10.3 %copy-start.1 = (bf16[5,2,256,512]{3,2,1,0:T(8,128)(2,1)S(1)}, bf16[5,2,256,512]{3,2,1,0:T(8,128)(2,1)}, u32[]{:S(2)}) copy-start(bf16[5,2,256,512]{3,2,1,0:T(8,128)(2,1)} %param.8) | copy-start | bytes 7864324
  10.3 4.2 %collective-permute-start = (bf16[2,256,128]{2,1,0:T(8,128)(2,1)}, bf16[2,256,128]{2,1,0:T(8,128)(2,1)S(1)}, u32[]{:S(2)}, u32[]{:S(2)}) collective-permute-start(bf16[2,256,128]{2,1,0:T(8,128)(2,1)} %leaf.1), channel_id=1, source_target_pairs={{0,1},{1,0},{2,3},{3,2},{4,5},{5,4},{6,7},{7,6},{8,9},{9,8},{10,11... | collective-permute-start | bytes 393224 | tf_op jit(solution)/shard_map/ppermute | solution.py:18
  10.3 2.6 %copy-start.5 = (bf16[2,256,128]{2,1,0:T(8,128)(2,1)S(1)}, bf16[2,256,128]{2,1,0:T(8,128)(2,1)}, u32[]{:S(2)}) copy-start(bf16[2,256,128]{2,1,0:T(8,128)(2,1)} %leaf.1) | copy-start | bytes 393220
  11.7 1.5 %copy-start.4 = (bf16[2,256,512]{2,1,0:T(8,128)(2,1)S(1)}, bf16[2,256,512]{2,1,0:T(8,128)(2,1)}, u32[]{:S(2)}) copy-start(bf16[2,256,512]{2,1,0:T(8,128)(2,1)} %get-tuple-element.9) | copy-start | bytes 1572868
  11.7 1.6 %copy-start.3 = (bf16[2,256,512]{2,1,0:T(8,128)(2,1)S(1)}, bf16[2,256,512]{2,1,0:T(8,128)(2,1)}, u32[]{:S(2)}) copy-start(bf16[2,256,512]{2,1,0:T(8,128)(2,1)} %get-tuple-element.6) | copy-start | bytes 1572868
  12.9 1.1 %copy-start.2 = (bf16[2,256,512]{2,1,0:T(8,128)(2,1)S(1)}, bf16[2,256,512]{2,1,0:T(8,128)(2,1)}, u32[]{:S(2)}) copy-start(bf16[2,256,512]{2,1,0:T(8,128)(2,1)} %get-tuple-element.7) | copy-start | bytes 1572868
  15.2 6.0 %collective-permute-start.1 = (bf16[2,256,128]{2,1,0:T(8,128)(2,1)S(1)}, bf16[2,256,128]{2,1,0:T(8,128)(2,1)S(1)}, u32[]{:S(2)}, u32[]{:S(2)}) collective-permute-start(bf16[2,256,128]{2,1,0:T(8,128)(2,1)S(1)} %fusion.34), channel_id=1, source_target_pairs={{0,2},{2,0},{1,3},{3,1},{4,6},{6,4},{5,7},{7,5},{8,10},{10,8},{9,1... | collective-permute-start | bytes 393224 | tf_op jit(solution)/shard_map/ppermute | solution.py:18
  21.9 8.7 %collective-permute-start.2 = (bf16[2,256,128]{2,1,0:T(8,128)(2,1)S(1)}, bf16[2,256,128]{2,1,0:T(8,128)(2,1)S(1)}, u32[]{:S(2)}, u32[]{:S(2)}) collective-permute-start(bf16[2,256,128]{2,1,0:T(8,128)(2,1)S(1)} %fusion.35), channel_id=1, source_target_pairs={{0,4},{4,0},{1,5},{5,1},{2,6},{6,2},{3,7},{7,3},{8,12},{12,8},{9,1... | collective-permute-start | bytes 393224 | tf_op jit(solution)/shard_map/ppermute | solution.py:18
  31.4 12.2 %collective-permute-start.3 = (bf16[2,256,128]{2,1,0:T(8,128)(2,1)S(1)}, bf16[2,256,128]{2,1,0:T(8,128)(2,1)S(1)}, u32[]{:S(2)}, u32[]{:S(2)}) collective-permute-start(bf16[2,256,128]{2,1,0:T(8,128)(2,1)S(1)} %fusion.36), channel_id=1, source_target_pairs={{0,8},{8,0},{1,9},{9,1},{2,10},{10,2},{3,11},{11,3},{4,12},{12,4},... | collective-permute-start | bytes 393224 | tf_op jit(solution)/shard_map/ppermute | solution.py:18
  44.4 5.1 %collective-permute-start.4 = (bf16[2,256,128]{2,1,0:T(8,128)(2,1)S(1)}, bf16[2,256,128]{2,1,0:T(8,128)(2,1)S(1)}, u32[]{:S(2)}, u32[]{:S(2)}) collective-permute-start(bf16[2,256,128]{2,1,0:T(8,128)(2,1)S(1)} %fusion.37), channel_id=1, source_target_pairs={{0,16},{16,0},{1,17},{17,1},{2,18},{18,2},{3,19},{19,3},{4,20},{20... | collective-permute-start | bytes 393224 | tf_op jit(solution)/shard_map/ppermute | solution.py:18
  50.4 23.6 %copy-start = (bf16[2,256,3072]{2,1,0:T(8,128)(2,1)S(1)}, bf16[2,256,3072]{2,1,0:T(8,128)(2,1)}, u32[]{:S(2)}) copy-start(bf16[2,256,3072]{2,1,0:T(8,128)(2,1)} %param.9) | copy-start | bytes 9437188

commit v2 on v0

v2 whole, which is shorter than its diff:
```python
import functools

import jax
import jax.numpy as jnp
from jax import lax
from jax.experimental import pallas as pl
from jax.experimental.pallas import tpu as pltpu
from jax.sharding import PartitionSpec as P


def swap(block, axis, mask):
    count = lax.axis_size(axis)
    return lax.ppermute(block, axis, [(place, place ^ mask) for place in range(count)])


def leaf_kernel(order_hbm, source_hbm, basis_hbm, out_ref, order_ref, source_ref, basis_ref, by_point_ref, *rest):
    ordered_refs, (order_done, source_done, basis_done) = rest[:-3], rest[-3:]
    _, width, points = source_ref.shape
    rank = basis_ref.shape[1]
    chunk = ordered_refs[0].shape[0] // 2
    order_copy = pltpu.make_async_copy(order_hbm, order_ref, order_done)
    source_copies = [
        pltpu.make_async_copy(source_hbm.at[part], source_ref.at[part], source_done.at[part])
        for part in range(2)
    ]
    basis_copies = [
        pltpu.make_async_copy(basis_hbm.at[part], basis_ref.at[part], basis_done.at[part])
        for part in range(2)
    ]
    for copy in (order_copy, *source_copies, *basis_copies):
        copy.start()
    for part in range(2):
        source_copies[part].wait()
        for start in range(0, points, 256):
            block = source_ref[part, :, start : start + 256].astype(jnp.float32)
            by_point_ref[pl.ds(2 * start + part, 256, stride=2), :] = block.T
    order_copy.wait()
    total = None
    for at in range(len(ordered_refs) + 1):
        if at == 1:
            for copy in basis_copies:
                copy.wait()
        if at < len(ordered_refs):
            for row in range(chunk):
                point = pl.multiple_of(2 * order_ref[0, at * chunk + row], 2)
                ordered_refs[at][2 * row : 2 * row + 2, :] = by_point_ref[pl.ds(point, 2), :]
        if at > 0:
            ordered = jnp.concatenate(
                [
                    ordered_refs[at - 1][pl.ds(part, chunk, stride=2), :].astype(jnp.bfloat16)
                    for part in range(2)
                ],
                axis=1,
            )
            basis = basis_ref[:, :, (at - 1) * chunk : at * chunk].reshape(2 * rank, chunk)
            term = jnp.dot(basis, ordered, preferred_element_type=jnp.float32)
            total = term if total is None else total + term
    out_ref[:rank] = (total[:rank, :width] - total[rank:, width:]).astype(jnp.bfloat16)
    out_ref[rank:] = (total[:rank, width:] + total[rank:, :width]).astype(jnp.bfloat16)


def leaf_coefficients(excitation, point_order, projection, chunk=512):
    _, width, points = excitation.shape
    rank = projection.shape[1]
    point_order, excitation, projection = (
        pltpu.with_memory_space_constraint(array, pltpu.HBM)
        for array in (point_order, excitation, projection)
    )
    return pl.pallas_call(
        leaf_kernel,
        in_specs=[pl.BlockSpec(memory_space=pltpu.HBM)] * 3,
        out_specs=pl.BlockSpec(memory_space=pltpu.VMEM),
        out_shape=jax.ShapeDtypeStruct((2 * rank, width), jnp.bfloat16),
        scratch_shapes=[
            pltpu.SMEM((1, points), jnp.int32),
            pltpu.VMEM(excitation.shape, jnp.bfloat16),
            pltpu.VMEM(projection.shape, jnp.bfloat16),
            pltpu.VMEM((2 * points, width), jnp.float32),
            *[pltpu.VMEM((2 * chunk, width), jnp.float32)] * (points // chunk),
            pltpu.SemaphoreType.DMA,
            pltpu.SemaphoreType.DMA((2,)),
            pltpu.SemaphoreType.DMA((2,)),
        ],
        compiler_params=pltpu.CompilerParams(vmem_limit_bytes=24 << 20),
        name="leaf",
    )(point_order, excitation, projection)


def expand_kernel(total_ref, basis_ref, out_hbm, left_ref, out_ref, done):
    rank, points = basis_ref.shape[1:]
    width = total_ref.shape[1]
    chunk = points // done.shape[0]
    left_ref[:width] = total_ref[:rank].T
    left_ref[width:] = total_ref[rank:].T
    left = left_ref[...]
    copies = []
    for at in range(points // chunk):
        here = pl.ds(at * chunk, chunk)
        by_real = jnp.dot(left, basis_ref[0, :, here], preferred_element_type=jnp.float32)
        by_imag = jnp.dot(left, basis_ref[1, :, here], preferred_element_type=jnp.float32)
        out_ref[0, :, here] = (by_real[:width] - by_imag[width:]).astype(jnp.bfloat16)
        out_ref[1, :, here] = (by_real[width:] + by_imag[:width]).astype(jnp.bfloat16)
        copies.append(
            pltpu.make_async_copy(out_ref.at[:, :, here], out_hbm.at[:, :, here], done.at[at])
        )
        copies[-1].start()
    for copy in copies:
        copy.wait()


def expanded(total, expansion, chunk=512):
    _, rank, points = expansion.shape
    width = total.shape[1]
    return pl.pallas_call(
        expand_kernel,
        in_specs=[pl.BlockSpec(memory_space=pltpu.VMEM)] * 2,
        out_specs=pl.BlockSpec(memory_space=pltpu.HBM),
        out_shape=jax.ShapeDtypeStruct((2, width, points), jnp.bfloat16),
        scratch_shapes=[
            pltpu.VMEM((2 * width, rank), jnp.bfloat16),
            pltpu.VMEM((2, width, points), jnp.bfloat16),
            pltpu.SemaphoreType.DMA((points // chunk,)),
        ],
        compiler_params=pltpu.CompilerParams(vmem_limit_bytes=16 << 20),
        name="expand",
    )(total, expansion)


def level_kernel(coefficients_ref, matrix_ref, own_ref, other_ref, *, level):
    rank = matrix_ref.shape[2]
    width = coefficients_ref.shape[1]
    upper = lax.axis_index("leaf") >> level & 1
    own_half = pl.ds(pl.multiple_of(upper * rank, rank), rank)
    other_half = pl.ds(pl.multiple_of((1 - upper) * rank, rank), rank)
    matrix = matrix_ref[0, :, :, own_half].reshape(2 * rank, rank)
    coefficients = jnp.concatenate(
        (coefficients_ref[:rank], coefficients_ref[rank:]), axis=1
    )
    term = jnp.dot(matrix, coefficients, preferred_element_type=jnp.float32)
    own_ref[:rank] = term[:rank, :width] - term[rank:, width:]
    own_ref[rank:] = term[:rank, width:] + term[rank:, :width]
    real = matrix_ref[0, 0, :, other_half]
    imag = matrix_ref[0, 1, :, other_half]
    other_ref[:rank, :rank] = real
    other_ref[:rank, rank:] = -imag
    other_ref[rank:, :rank] = imag
    other_ref[rank:, rank:] = real


def own_part(coefficients, transfer, level):
    rank = transfer.shape[2]
    whole = lambda _: (0, 0)
    return pl.pallas_call(
        functools.partial(level_kernel, level=level),
        grid=(1,),
        in_specs=[
            pl.BlockSpec(coefficients.shape, whole),
            pl.BlockSpec((1, 2, rank, 2 * rank), lambda _: (level, 0, 0, 0)),
        ],
        out_specs=[
            pl.BlockSpec(coefficients.shape, whole),
            pl.BlockSpec((2 * rank, 2 * rank), whole),
        ],
        out_shape=[
            jax.ShapeDtypeStruct(coefficients.shape, jnp.float32),
            jax.ShapeDtypeStruct((2 * rank, 2 * rank), jnp.bfloat16),
        ],
        compiler_params=pltpu.CompilerParams(vmem_limit_bytes=8 << 20),
        cost_estimate=pl.CostEstimate(
            flops=8 * rank * rank * coefficients.shape[1],
            bytes_accessed=8 * rank * rank * 2,
            transcendentals=0,
        ),
        name="own_part",
    )(coefficients, transfer)


def per_device(excitation, point_order, projection, transfer, expansion):
    coefficients = leaf_coefficients(excitation, point_order, projection)
    for level in range(transfer.shape[0]):
        partner = swap(coefficients, "leaf", 1 << level)
        own_term, other = own_part(coefficients, transfer, level)
        other_term = jnp.dot(other, partner, preferred_element_type=jnp.float32)
        coefficients = (own_term + other_term).astype(jnp.bfloat16)
    pair = swap(coefficients, "panel", 1)
    coefficients = (coefficients.astype(jnp.float32) + pair.astype(jnp.float32)).astype(jnp.bfloat16)
    across = [swap(coefficients, "panel", mask) for mask in (4, 2, 6)]
    total = coefficients.astype(jnp.float32)
    for term in across:
        total = total + term.astype(jnp.float32)
    return expanded(total.astype(jnp.bfloat16), expansion)


def solution(mesh):
    in_specs = (
        P(None, None, ("panel", "leaf")),
        P(("panel", "leaf"), None),
        P(None, None, ("panel", "leaf")),
        P(None, None, ("panel", "leaf"), None),
        P(None, None, ("panel", "leaf")),
    )
    out_specs = P(None, None, ("panel", "leaf"))
    return jax.shard_map(
        per_device, mesh=mesh, in_specs=in_specs, out_specs=out_specs, check_vma=False
    )
```

time: 101 us -> 60.8 us (0.60)
  the two profiles are of different devices: /device:TPU:96 before, /device:TPU:18 now
where the time goes in v2:
time: 60.8 us
  waiting for transfers between devices  33.7 us (55%)
  starting transfers between devices  16.8 us (28%)
  Pallas kernels  8.39 us (14%)
  matrix products  1.46 us (2%)
    ppermute x9, waiting for transfers between devices, swap(): lax.ppermute(block, axis, [(place, place ^ mask) for place in range(count)])  33.7 us
    ppermute x9, starting transfers between devices, swap(): lax.ppermute(block, axis, [(place, place ^ mask) for place in range(count)])  16.8 us
    pallas_call x1, Pallas kernels, leaf_coefficients(): pl.pallas_call(leaf_kernel, in_specs=[pl.BlockSpec(memory_space=pltpu.HBM...  5.51 us
    pallas_call x1, Pallas kernels, expanded(): pl.pallas_call(expand_kernel, in_specs=[pl.BlockSpec(memory_space=pltpu.V...  1.76 us
    dot_general x5, matrix products, per_device(): other_term = jnp.dot(other, partner, preferred_element_type=jnp.float32)  1.46 us
  transfers between devices with their start and end apart: 9, of which 9 were waited for; matrix products, arithmetic and copies ran while one was open for 0% of the time, Pallas kernels for 2%

profile of v2, /device:TPU:18, one launch (start us, length us, event | category | flops | bytes accessed | tf_op | source)
XLA Modules:
  0.0 60.8 jit_solution(14960408385625435815)
XLA Ops:
  0.0 5.5 %leaf.1.coefficients_ref = bf16[512,128]{1,0:T(8,128)(2,1)S(1)} custom-call(s32[1,3072]{1,0:T(1,128)} %order_hbm.1, bf16[2,128,3072]{2,1,0:T(8,128)(2,1)} %source_hbm.1, bf16[2,256,3072]{2,1,0:T(8,128)(2,1)} %basis_hbm.1), custom_call_target="tpu_custom_call" | custom-call | tf_op jit(solution)/shard_map/leaf/pallas_call | solution.py:69
  5.5 0.1 collective-permute-start
  5.6 0.2 own_part.5
  5.9 1.1 %collective-permute-done = bf16[512,128]{1,0:T(8,128)(2,1)S(1)} collective-permute-done((bf16[512,128]{1,0:T(8,128)(2,1)S(1)}, bf16[512,128]{1,0:T(8,128)(2,1)S(1)}, u32[]{:S(2)}, u32[]{:S(2)}) %collective-permute-start) | collective-permute-done | bytes 131104 | tf_op jit(solution)/shard_map/ppermute | solution.py:13
  7.0 0.3 fusion.coefficients_ref
  7.3 2.0 %collective-permute-start.1 = (bf16[512,128]{1,0:T(8,128)(2,1)S(1)}, bf16[512,128]{1,0:T(8,128)(2,1)S(1)}, u32[]{:S(2)}, u32[]{:S(2)}) collective-permute-start(bf16[512,128]{1,0:T(8,128)(2,1)S(1)} %fusion.coefficients_ref), channel_id=1, source_target_pairs={{0,2},{1,3},{2,0},{3,1},{4,6},{5,7},{6,4},{7,5},{8,10},{9,11},{10,... | collective-permute-start | bytes 393224 | tf_op jit(solution)/shard_map/ppermute | solution.py:13
  9.3 0.2 own_part.6
  9.5 3.6 %collective-permute-done.1 = bf16[512,128]{1,0:T(8,128)(2,1)S(1)} collective-permute-done((bf16[512,128]{1,0:T(8,128)(2,1)S(1)}, bf16[512,128]{1,0:T(8,128)(2,1)S(1)}, u32[]{:S(2)}, u32[]{:S(2)}) %collective-permute-start.1) | collective-permute-done | bytes 131104 | tf_op jit(solution)/shard_map/ppermute | solution.py:13
  13.1 0.3 fusion.1
  13.4 3.4 %collective-permute-start.2 = (bf16[512,128]{1,0:T(8,128)(2,1)S(1)}, bf16[512,128]{1,0:T(8,128)(2,1)S(1)}, u32[]{:S(2)}, u32[]{:S(2)}) collective-permute-start(bf16[512,128]{1,0:T(8,128)(2,1)S(1)} %add_convert_fusion.5.coefficients_ref), channel_id=1, source_target_pairs={{0,4},{1,5},{2,6},{3,7},{4,0},{5,1},{6,2},{7,3},{8,12},{9,13},{10,... | collective-permute-start | bytes 393224 | tf_op jit(solution)/shard_map/ppermute | solution.py:13
  16.8 0.2 own_part.7
  17.0 5.7 %collective-permute-done.2 = bf16[512,128]{1,0:T(8,128)(2,1)S(1)} collective-permute-done((bf16[512,128]{1,0:T(8,128)(2,1)S(1)}, bf16[512,128]{1,0:T(8,128)(2,1)S(1)}, u32[]{:S(2)}, u32[]{:S(2)}) %collective-permute-start.2) | collective-permute-done | bytes 131104 | tf_op jit(solution)/shard_map/ppermute | solution.py:13
  22.7 0.3 fusion.2
  23.0 6.3 %collective-permute-start.3 = (bf16[512,128]{1,0:T(8,128)(2,1)S(1)}, bf16[512,128]{1,0:T(8,128)(2,1)S(1)}, u32[]{:S(2)}, u32[]{:S(2)}) collective-permute-start(bf16[512,128]{1,0:T(8,128)(2,1)S(1)} %add_convert_fusion.4.coefficients_ref), channel_id=1, source_target_pairs={{0,8},{1,9},{2,10},{3,11},{4,12},{5,13},{6,14},{7,15},{8,0},{9,1},... | collective-permute-start | bytes 393224 | tf_op jit(solution)/shard_map/ppermute | solution.py:13
  29.3 0.2 own_part.8
  29.6 5.8 %collective-permute-done.3 = bf16[512,128]{1,0:T(8,128)(2,1)S(1)} collective-permute-done((bf16[512,128]{1,0:T(8,128)(2,1)S(1)}, bf16[512,128]{1,0:T(8,128)(2,1)S(1)}, u32[]{:S(2)}, u32[]{:S(2)}) %collective-permute-start.3) | collective-permute-done | bytes 131104 | tf_op jit(solution)/shard_map/ppermute | solution.py:13
  35.4 0.3 fusion.3
  35.7 0.0 copy-start.1
  35.7 1.4 %collective-permute-start.4 = (bf16[512,128]{1,0:T(8,128)(2,1)S(1)}, bf16[512,128]{1,0:T(8,128)(2,1)S(1)}, u32[]{:S(2)}, u32[]{:S(2)}) collective-permute-start(bf16[512,128]{1,0:T(8,128)(2,1)S(1)} %add_convert_fusion.3.coefficients_ref), channel_id=1, source_target_pairs={{0,16},{1,17},{2,18},{3,19},{4,20},{5,21},{6,22},{7,23},{8,24},{9,... | collective-permute-start | bytes 393224 | tf_op jit(solution)/shard_map/ppermute | solution.py:13
  37.1 0.2 own_part.9
  37.3 4.8 %collective-permute-done.4 = bf16[512,128]{1,0:T(8,128)(2,1)S(1)} collective-permute-done((bf16[512,128]{1,0:T(8,128)(2,1)S(1)}, bf16[512,128]{1,0:T(8,128)(2,1)S(1)}, u32[]{:S(2)}, u32[]{:S(2)}) %collective-permute-start.4) | collective-permute-done | bytes 131104 | tf_op jit(solution)/shard_map/ppermute | solution.py:13
  42.1 0.3 fusion.4
  42.4 0.1 collective-permute-start.5
  42.5 6.5 %collective-permute-done.5 = bf16[512,128]{1,0:T(8,128)(2,1)S(1)} collective-permute-done((bf16[512,128]{1,0:T(8,128)(2,1)S(1)}, bf16[512,128]{1,0:T(8,128)(2,1)S(1)}, u32[]{:S(2)}, u32[]{:S(2)}) %collective-permute-start.5) | collective-permute-done | bytes 131104 | tf_op jit(solution)/shard_map/ppermute | solution.py:13
  49.0 1.6 %collective-permute-start.8 = (bf16[512,128]{1,0:T(8,128)(2,1)S(1)}, bf16[512,128]{1,0:T(8,128)(2,1)S(1)}, u32[]{:S(2)}, u32[]{:S(2)}) collective-permute-start(bf16[512,128]{1,0:T(8,128)(2,1)S(1)} %add_convert_fusion.1), channel_id=1, source_target_pairs={{0,192},{32,224},{64,128},{96,160},{128,64},{160,96},{192,0},{224,... | collective-permute-start | bytes 393224 | tf_op jit(solution)/shard_map/ppermute | solution.py:13
  50.7 1.8 %collective-permute-start.7 = (bf16[512,128]{1,0:T(8,128)(2,1)S(1)}, bf16[512,128]{1,0:T(8,128)(2,1)S(1)}, u32[]{:S(2)}, u32[]{:S(2)}) collective-permute-start(bf16[512,128]{1,0:T(8,128)(2,1)S(1)} %add_convert_fusion.1), channel_id=1, source_target_pairs={{0,64},{32,96},{64,0},{96,32},{128,192},{160,224},{192,128},{224,1... | collective-permute-start | bytes 393224 | tf_op jit(solution)/shard_map/ppermute | solution.py:13
  52.4 0.2 collective-permute-start.6
  52.6 1.5 %collective-permute-done.8 = bf16[512,128]{1,0:T(8,128)(2,1)S(1)} collective-permute-done((bf16[512,128]{1,0:T(8,128)(2,1)S(1)}, bf16[512,128]{1,0:T(8,128)(2,1)S(1)}, u32[]{:S(2)}, u32[]{:S(2)}) %collective-permute-start.8) | collective-permute-done | bytes 131104 | tf_op jit(solution)/shard_map/ppermute | solution.py:13
  54.1 1.5 %collective-permute-done.7 = bf16[512,128]{1,0:T(8,128)(2,1)S(1)} collective-permute-done((bf16[512,128]{1,0:T(8,128)(2,1)S(1)}, bf16[512,128]{1,0:T(8,128)(2,1)S(1)}, u32[]{:S(2)}, u32[]{:S(2)}) %collective-permute-start.7) | collective-permute-done | bytes 131104 | tf_op jit(solution)/shard_map/ppermute | solution.py:13
  55.6 3.3 %collective-permute-done.6 = bf16[512,128]{1,0:T(8,128)(2,1)S(1)} collective-permute-done((bf16[512,128]{1,0:T(8,128)(2,1)S(1)}, bf16[512,128]{1,0:T(8,128)(2,1)S(1)}, u32[]{:S(2)}, u32[]{:S(2)}) %collective-permute-start.6) | collective-permute-done | bytes 131104 | tf_op jit(solution)/shard_map/ppermute | solution.py:13
  58.9 0.1 add_convert_fusion.total_ref
  59.0 1.8 %expand.1 = bf16[2,128,3072]{2,1,0:T(8,128)(2,1)} custom-call(bf16[512,128]{1,0:T(8,128)(2,1)S(1)} %add_convert_fusion.total_ref, bf16[2,256,3072]{2,1,0:T(8,128)(2,1)S(1)} %copy-done.1), custom_call_target="tpu_custom_call" | custom-call | tf_op jit(solution)/shard_map/expand/pallas_call | solution.py:114
  (8 shorter events, 0.2 us)
Async XLA Ops:
  0.0 5.6 %copy-start = (bf16[5,2,256,512]{3,2,1,0:T(8,128)(2,1)S(1)}, bf16[5,2,256,512]{3,2,1,0:T(8,128)(2,1)}, u32[]{:S(2)}) copy-start(bf16[5,2,256,512]{3,2,1,0:T(8,128)(2,1)} %matrix_ref.9) | copy-start | bytes 7864324
  5.5 1.4 %collective-permute-start = (bf16[512,128]{1,0:T(8,128)(2,1)S(1)}, bf16[512,128]{1,0:T(8,128)(2,1)S(1)}, u32[]{:S(2)}, u32[]{:S(2)}) collective-permute-start(bf16[512,128]{1,0:T(8,128)(2,1)S(1)} %leaf.1.coefficients_ref), channel_id=1, source_target_pairs={{0,1},{1,0},{2,3},{3,2},{4,5},{5,4},{6,7},{7,6},{8,9},{9,8},{10,11... | collective-permute-start | bytes 393224 | tf_op jit(solution)/shard_map/ppermute | solution.py:13
  7.3 5.8 %collective-permute-start.1 = (bf16[512,128]{1,0:T(8,128)(2,1)S(1)}, bf16[512,128]{1,0:T(8,128)(2,1)S(1)}, u32[]{:S(2)}, u32[]{:S(2)}) collective-permute-start(bf16[512,128]{1,0:T(8,128)(2,1)S(1)} %fusion.coefficients_ref), channel_id=1, source_target_pairs={{0,2},{1,3},{2,0},{3,1},{4,6},{5,7},{6,4},{7,5},{8,10},{9,11},{10,... | collective-permute-start | bytes 393224 | tf_op jit(solution)/shard_map/ppermute | solution.py:13
  13.4 9.3 %collective-permute-start.2 = (bf16[512,128]{1,0:T(8,128)(2,1)S(1)}, bf16[512,128]{1,0:T(8,128)(2,1)S(1)}, u32[]{:S(2)}, u32[]{:S(2)}) collective-permute-start(bf16[512,128]{1,0:T(8,128)(2,1)S(1)} %add_convert_fusion.5.coefficients_ref), channel_id=1, source_target_pairs={{0,4},{1,5},{2,6},{3,7},{4,0},{5,1},{6,2},{7,3},{8,12},{9,13},{10,... | collective-permute-start | bytes 393224 | tf_op jit(solution)/shard_map/ppermute | solution.py:13
  23.0 12.4 %collective-permute-start.3 = (bf16[512,128]{1,0:T(8,128)(2,1)S(1)}, bf16[512,128]{1,0:T(8,128)(2,1)S(1)}, u32[]{:S(2)}, u32[]{:S(2)}) collective-permute-start(bf16[512,128]{1,0:T(8,128)(2,1)S(1)} %add_convert_fusion.4.coefficients_ref), channel_id=1, source_target_pairs={{0,8},{1,9},{2,10},{3,11},{4,12},{5,13},{6,14},{7,15},{8,0},{9,1},... | collective-permute-start | bytes 393224 | tf_op jit(solution)/shard_map/ppermute | solution.py:13
  35.7 23.3 %copy-start.1 = (bf16[2,256,3072]{2,1,0:T(8,128)(2,1)S(1)}, bf16[2,256,3072]{2,1,0:T(8,128)(2,1)}, u32[]{:S(2)}) copy-start(bf16[2,256,3072]{2,1,0:T(8,128)(2,1)} %basis_ref.1) | copy-start | bytes 9437188
  35.7 6.4 %collective-permute-start.4 = (bf16[512,128]{1,0:T(8,128)(2,1)S(1)}, bf16[512,128]{1,0:T(8,128)(2,1)S(1)}, u32[]{:S(2)}, u32[]{:S(2)}) collective-permute-start(bf16[512,128]{1,0:T(8,128)(2,1)S(1)} %add_convert_fusion.3.coefficients_ref), channel_id=1, source_target_pairs={{0,16},{1,17},{2,18},{3,19},{4,20},{5,21},{6,22},{7,23},{8,24},{9,... | collective-permute-start | bytes 393224 | tf_op jit(solution)/shard_map/ppermute | solution.py:13
  42.4 6.6 %collective-permute-start.5 = (bf16[512,128]{1,0:T(8,128)(2,1)S(1)}, bf16[512,128]{1,0:T(8,128)(2,1)S(1)}, u32[]{:S(2)}, u32[]{:S(2)}) collective-permute-start(bf16[512,128]{1,0:T(8,128)(2,1)S(1)} %add_convert_fusion.2), channel_id=1, source_target_pairs={{0,32},{32,0},{64,96},{96,64},{128,160},{160,128},{192,224},{224,1... | collective-permute-start | bytes 393224 | tf_op jit(solution)/shard_map/ppermute | solution.py:13
  49.0 5.1 %collective-permute-start.8 = (bf16[512,128]{1,0:T(8,128)(2,1)S(1)}, bf16[512,128]{1,0:T(8,128)(2,1)S(1)}, u32[]{:S(2)}, u32[]{:S(2)}) collective-permute-start(bf16[512,128]{1,0:T(8,128)(2,1)S(1)} %add_convert_fusion.1), channel_id=1, source_target_pairs={{0,192},{32,224},{64,128},{96,160},{128,64},{160,96},{192,0},{224,... | collective-permute-start | bytes 393224 | tf_op jit(solution)/shard_map/ppermute | solution.py:13
  50.7 5.0 %collective-permute-start.7 = (bf16[512,128]{1,0:T(8,128)(2,1)S(1)}, bf16[512,128]{1,0:T(8,128)(2,1)S(1)}, u32[]{:S(2)}, u32[]{:S(2)}) collective-permute-start(bf16[512,128]{1,0:T(8,128)(2,1)S(1)} %add_convert_fusion.1), channel_id=1, source_target_pairs={{0,64},{32,96},{64,0},{96,32},{128,192},{160,224},{192,128},{224,1... | collective-permute-start | bytes 393224 | tf_op jit(solution)/shard_map/ppermute | solution.py:13
  52.4 6.5 %collective-permute-start.6 = (bf16[512,128]{1,0:T(8,128)(2,1)S(1)}, bf16[512,128]{1,0:T(8,128)(2,1)S(1)}, u32[]{:S(2)}, u32[]{:S(2)}) collective-permute-start(bf16[512,128]{1,0:T(8,128)(2,1)S(1)} %add_convert_fusion.1), channel_id=1, source_target_pairs={{0,128},{32,160},{64,192},{96,224},{128,0},{160,32},{192,64},{224,... | collective-permute-start | bytes 393224 | tf_op jit(solution)/shard_map/ppermute | solution.py:13

commit v3 on v2

--- a/solution.py
+++ b/solution.py
@@ -126,69 +126,100 @@
     )(total, expansion)
 
 
-def level_kernel(coefficients_ref, matrix_ref, own_ref, other_ref, *, level):
-    rank = matrix_ref.shape[2]
-    width = coefficients_ref.shape[1]
+def half_of(transfer_ref, level, own):
+    rank = transfer_ref.shape[2]
     upper = lax.axis_index("leaf") >> level & 1
-    own_half = pl.ds(pl.multiple_of(upper * rank, rank), rank)
-    other_half = pl.ds(pl.multiple_of((1 - upper) * rank, rank), rank)
-    matrix = matrix_ref[0, :, :, own_half].reshape(2 * rank, rank)
-    coefficients = jnp.concatenate(
-        (coefficients_ref[:rank], coefficients_ref[rank:]), axis=1
-    )
-    term = jnp.dot(matrix, coefficients, preferred_element_type=jnp.float32)
-    own_ref[:rank] = term[:rank, :width] - term[rank:, width:]
-    own_ref[rank:] = term[:rank, width:] + term[rank:, :width]
-    real = matrix_ref[0, 0, :, other_half]
-    imag = matrix_ref[0, 1, :, other_half]
-    other_ref[:rank, :rank] = real
-    other_ref[:rank, rank:] = -imag
-    other_ref[rank:, :rank] = imag
-    other_ref[rank:, rank:] = real
-
-
-def own_part(coefficients, transfer, level):
-    rank = transfer.shape[2]
-    whole = lambda _: (0, 0)
+    side = upper if own else 1 - upper
+    return transfer_ref[level, :, :, pl.ds(pl.multiple_of(side * rank, rank), rank)]
+
+
+def complex_product(matrix, coefficients):
+    _, rows, rank = matrix.shape
+    width = coefficients.shape[1]
+    side_by_side = jnp.concatenate((coefficients[:rank], coefficients[rank:]), axis=1)
+    term = jnp.dot(
+        matrix.reshape(2 * rows, rank), side_by_side, preferred_element_type=jnp.float32
+    )
+    return term[:rows, :width] - term[rows:, width:], term[:rows, width:] + term[rows:, :width]
+
+
+def put(out_ref, parts):
+    rank = out_ref.shape[0] // 2
+    out_ref[:rank] = parts[0].astype(out_ref.dtype)
+    out_ref[rank:] = parts[1].astype(out_ref.dtype)
+
+
+def own_kernel(coefficients_ref, transfer_ref, own_ref, *sent_refs, level, sent_level):
+    put(own_ref, complex_product(half_of(transfer_ref, level, True), coefficients_ref[...]))
+    for sent_ref in sent_refs:
+        sent_ref[...] = half_of(transfer_ref, sent_level, False)
+
+
+def partner_kernel(own_ref, partner_ref, transfer_ref, out_ref, *, level):
+    rank = transfer_ref.shape[2]
+    real, imag = complex_product(half_of(transfer_ref, level, False), partner_ref[...])
+    put(out_ref, (own_ref[:rank] + real, own_ref[rank:] + imag))
+
+
+def both_kernel(coefficients_ref, foreign_ref, transfer_ref, own_ref, cross_ref, *, level):
+    coefficients = coefficients_ref[...]
+    put(own_ref, complex_product(half_of(transfer_ref, level, True), coefficients))
+    put(cross_ref, complex_product(foreign_ref[...], coefficients))
+
+
+def small_call(kernel, name, out_shape, *operands):
     return pl.pallas_call(
-        functools.partial(level_kernel, level=level),
-        grid=(1,),
-        in_specs=[
-            pl.BlockSpec(coefficients.shape, whole),
-            pl.BlockSpec((1, 2, rank, 2 * rank), lambda _: (level, 0, 0, 0)),
-        ],
-        out_specs=[
-            pl.BlockSpec(coefficients.shape, whole),
-            pl.BlockSpec((2 * rank, 2 * rank), whole),
-        ],
-        out_shape=[
-            jax.ShapeDtypeStruct(coefficients.shape, jnp.float32),
-            jax.ShapeDtypeStruct((2 * rank, 2 * rank), jnp.bfloat16),
-        ],
+        kernel,
+        in_specs=[pl.BlockSpec(memory_space=pltpu.VMEM)] * len(operands),
+        out_specs=jax.tree.map(lambda _: pl.BlockSpec(memory_space=pltpu.VMEM), out_shape),
+        out_shape=out_shape,
         compiler_params=pltpu.CompilerParams(vmem_limit_bytes=8 << 20),
-        cost_estimate=pl.CostEstimate(
-            flops=8 * rank * rank * coefficients.shape[1],
-            bytes_accessed=8 * rank * rank * 2,
-            transcendentals=0,
-        ),
-        name="own_part",
-    )(coefficients, transfer)
+        cost_estimate=pl.CostEstimate(flops=1 << 26, bytes_accessed=1 << 19, transcendentals=0),
+        name=name,
+    )(*operands)
 
 
 def per_device(excitation, point_order, projection, transfer, expansion):
     coefficients = leaf_coefficients(excitation, point_order, projection)
-    for level in range(transfer.shape[0]):
+    levels, _, rank, _ = transfer.shape
+    last = levels - 1
+    shape = coefficients.shape
+    node = jax.ShapeDtypeStruct(shape, jnp.bfloat16)
+    for level in range(last):
         partner = swap(coefficients, "leaf", 1 << level)
-        own_term, other = own_part(coefficients, transfer, level)
-        other_term = jnp.dot(other, partner, preferred_element_type=jnp.float32)
-        coefficients = (own_term + other_term).astype(jnp.bfloat16)
-    pair = swap(coefficients, "panel", 1)
-    coefficients = (coefficients.astype(jnp.float32) + pair.astype(jnp.float32)).astype(jnp.bfloat16)
-    across = [swap(coefficients, "panel", mask) for mask in (4, 2, 6)]
-    total = coefficients.astype(jnp.float32)
+        out_shape = [jax.ShapeDtypeStruct(shape, jnp.float32)]
+        if level == 1:
+            out_shape.append(jax.ShapeDtypeStruct((2, rank, rank), jnp.bfloat16))
+        own_term, *sent = small_call(
+            functools.partial(own_kernel, level=level, sent_level=last),
+            "own", out_shape, coefficients, transfer,
+        )
+        if sent:
+            foreign = swap(sent[0], "leaf", 1 << last)
+        coefficients = small_call(
+            functools.partial(partner_kernel, level=level),
+            "partner", node, own_term, partner, transfer,
+        )
+    own, cross = small_call(
+        functools.partial(both_kernel, level=last), "both", [node, node],
+        coefficients, foreign, transfer,
+    )
+    leaf_count = lax.axis_size("leaf")
+    around = [
+        swap(own, "panel", 1),
+        swap(cross, "leaf", 1 << last),
+        swap(cross, ("panel", "leaf"), leaf_count | 1 << last),
+    ]
+    total = own.astype(jnp.float32)
+    for term in around:
+        total = total + term.astype(jnp.float32)
+    total = total.astype(jnp.bfloat16)
+    across = [swap(total, "panel", mask) for mask in (4, 2, 6)]
+    total = total.astype(jnp.float32)
     for term in across:
         total = total + term.astype(jnp.float32)
-    return expanded(total.astype(jnp.bfloat16), expansion)
+    total = total.astype(jnp.bfloat16)
+    return expanded(total, expansion)
 
 
 def solution(mesh):

time: 60.8 us -> 57 us (0.938)
  the two profiles are of different devices: /device:TPU:18 before, /device:TPU:2 now
where the time goes in v3:
time: 57 us; the launch traced here: 56.9 us
  waiting for transfers between devices  26.1 us (46%)
  starting transfers between devices  21.3 us (37%)
  Pallas kernels  9.34 us (16%)
    ppermute x11, waiting for transfers between devices, swap(): lax.ppermute(block, axis, [(place, place ^ mask) for place in range(count)])  26.1 us
    ppermute x11, starting transfers between devices, swap(): lax.ppermute(block, axis, [(place, place ^ mask) for place in range(count)])  21.3 us
    pallas_call x1, Pallas kernels, leaf_coefficients(): pl.pallas_call(leaf_kernel, in_specs=[pl.BlockSpec(memory_space=pltpu.HBM...  5.51 us
    pallas_call x9, Pallas kernels, small_call(): pl.pallas_call(kernel, in_specs=[pl.BlockSpec(memory_space=pltpu.VMEM)] *...  2.07 us
    pallas_call x1, Pallas kernels, expanded(): pl.pallas_call(expand_kernel, in_specs=[pl.BlockSpec(memory_space=pltpu.V...  1.76 us
  transfers between devices with their start and end apart: 11, of which 9 were waited for; matrix products, arithmetic and copies ran while one was open for 0% of the time, Pallas kernels for 2%

profile of v3, /device:TPU:2, one launch (start us, length us, event | category | flops | bytes accessed | tf_op | source)
XLA Modules:
  0.0 56.9 jit_solution(12947615432184072780)
XLA Ops:
  0.0 5.5 %leaf.1.coefficients_ref = bf16[512,128]{1,0:T(8,128)(2,1)S(1)} custom-call(s32[1,3072]{1,0:T(1,128)} %order_hbm.1, bf16[2,128,3072]{2,1,0:T(8,128)(2,1)} %source_hbm.1, bf16[2,256,3072]{2,1,0:T(8,128)(2,1)} %basis_hbm.1), custom_call_target="tpu_custom_call" | custom-call | tf_op jit(solution)/shard_map/leaf/pallas_call | solution.py:69
  5.5 0.1 collective-permute-start
  5.6 0.2 own.4.own_ref
  5.9 1.1 %collective-permute-done.partner_ref = bf16[512,128]{1,0:T(8,128)(2,1)S(1)} collective-permute-done((bf16[512,128]{1,0:T(8,128)(2,1)S(1)}, bf16[512,128]{1,0:T(8,128)(2,1)S(1)}, u32[]{:S(2)}, u32[]{:S(2)}) %collective-permute-start) | collective-permute-done | bytes 131104 | tf_op jit(solution)/shard_map/ppermute | solution.py:13
  7.0 0.2 partner.4.coefficients_ref
  7.2 2.0 %collective-permute-start.1 = (bf16[512,128]{1,0:T(8,128)(2,1)S(1)}, bf16[512,128]{1,0:T(8,128)(2,1)S(1)}, u32[]{:S(2)}, u32[]{:S(2)}) collective-permute-start(bf16[512,128]{1,0:T(8,128)(2,1)S(1)} %partner.4.coefficients_ref), channel_id=1, source_target_pairs={{0,2},{1,3},{2,0},{3,1},{4,6},{5,7},{6,4},{7,5},{8,10},{9,11},{10,... | collective-permute-start | bytes 393224 | tf_op jit(solution)/shard_map/ppermute | solution.py:13
  9.2 0.2 own.5
  9.4 3.6 %collective-permute-done.1.partner_ref = bf16[512,128]{1,0:T(8,128)(2,1)S(1)} collective-permute-done((bf16[512,128]{1,0:T(8,128)(2,1)S(1)}, bf16[512,128]{1,0:T(8,128)(2,1)S(1)}, u32[]{:S(2)}, u32[]{:S(2)}) %collective-permute-start.1) | collective-permute-done | bytes 131104 | tf_op jit(solution)/shard_map/ppermute | solution.py:13
  13.0 0.2 partner.5.coefficients_ref
  13.2 3.4 %collective-permute-start.2 = (bf16[512,128]{1,0:T(8,128)(2,1)S(1)}, bf16[512,128]{1,0:T(8,128)(2,1)S(1)}, u32[]{:S(2)}, u32[]{:S(2)}) collective-permute-start(bf16[512,128]{1,0:T(8,128)(2,1)S(1)} %partner.5.coefficients_ref), channel_id=1, source_target_pairs={{0,4},{1,5},{2,6},{3,7},{4,0},{5,1},{6,2},{7,3},{8,12},{9,13},{10,... | collective-permute-start | bytes 393224 | tf_op jit(solution)/shard_map/ppermute | solution.py:13
  16.6 1.6 %collective-permute-start.4 = (bf16[2,256,256]{2,1,0:T(8,128)(2,1)S(1)}, bf16[2,256,256]{2,1,0:T(8,128)(2,1)S(1)}, u32[]{:S(2)}, u32[]{:S(2)}) collective-permute-start(bf16[2,256,256]{2,1,0:T(8,128)(2,1)S(1)} %get-tuple-element.10), channel_id=1, source_target_pairs={{0,16},{1,17},{2,18},{3,19},{4,20},{5,21},{6,22},{7,23},{8,24},{9,... | collective-permute-start | bytes 786440 | tf_op jit(solution)/shard_map/ppermute | solution.py:13
  18.2 0.2 own.6.own_ref
  18.4 4.2 %collective-permute-done.2.partner_ref = bf16[512,128]{1,0:T(8,128)(2,1)S(1)} collective-permute-done((bf16[512,128]{1,0:T(8,128)(2,1)S(1)}, bf16[512,128]{1,0:T(8,128)(2,1)S(1)}, u32[]{:S(2)}, u32[]{:S(2)}) %collective-permute-start.2) | collective-permute-done | bytes 131104 | tf_op jit(solution)/shard_map/ppermute | solution.py:13
  22.5 0.2 partner.6.coefficients_ref
  22.8 6.3 %collective-permute-start.3 = (bf16[512,128]{1,0:T(8,128)(2,1)S(1)}, bf16[512,128]{1,0:T(8,128)(2,1)S(1)}, u32[]{:S(2)}, u32[]{:S(2)}) collective-permute-start(bf16[512,128]{1,0:T(8,128)(2,1)S(1)} %partner.6.coefficients_ref), channel_id=1, source_target_pairs={{0,8},{1,9},{2,10},{3,11},{4,12},{5,13},{6,14},{7,15},{8,0},{9,1},... | collective-permute-start | bytes 393224 | tf_op jit(solution)/shard_map/ppermute | solution.py:13
  29.1 0.2 own.7.own_ref
  29.3 5.8 %collective-permute-done.3.partner_ref = bf16[512,128]{1,0:T(8,128)(2,1)S(1)} collective-permute-done((bf16[512,128]{1,0:T(8,128)(2,1)S(1)}, bf16[512,128]{1,0:T(8,128)(2,1)S(1)}, u32[]{:S(2)}, u32[]{:S(2)}) %collective-permute-start.3) | collective-permute-done | bytes 131104 | tf_op jit(solution)/shard_map/ppermute | solution.py:13
  35.1 0.2 partner.7.coefficients_ref
  35.4 0.3 both.1
  35.7 3.3 %collective-permute-start.5 = (bf16[512,128]{1,0:T(8,128)(2,1)S(1)}, bf16[512,128]{1,0:T(8,128)(2,1)S(1)}, u32[]{:S(2)}, u32[]{:S(2)}) collective-permute-start(bf16[512,128]{1,0:T(8,128)(2,1)S(1)} %get-tuple-element.11), channel_id=1, source_target_pairs={{0,32},{32,0},{64,96},{96,64},{128,160},{160,128},{192,224},{224,1... | collective-permute-start | bytes 393224 | tf_op jit(solution)/shard_map/ppermute | solution.py:13
  38.9 1.1 %collective-permute-start.7 = (bf16[512,128]{1,0:T(8,128)(2,1)S(1)}, bf16[512,128]{1,0:T(8,128)(2,1)S(1)}, u32[]{:S(2)}, u32[]{:S(2)}) collective-permute-start(bf16[512,128]{1,0:T(8,128)(2,1)S(1)} %get-tuple-element.12), channel_id=1, source_target_pairs={{0,48},{1,49},{2,50},{3,51},{4,52},{5,53},{6,54},{7,55},{8,56},{9,... | collective-permute-start | bytes 393224 | tf_op jit(solution)/shard_map/ppermute | solution.py:13
  40.0 2.6 %collective-permute-done.5 = bf16[512,128]{1,0:T(8,128)(2,1)S(1)} collective-permute-done((bf16[512,128]{1,0:T(8,128)(2,1)S(1)}, bf16[512,128]{1,0:T(8,128)(2,1)S(1)}, u32[]{:S(2)}, u32[]{:S(2)}) %collective-permute-start.5) | collective-permute-done | bytes 131104 | tf_op jit(solution)/shard_map/ppermute | solution.py:13
  42.6 2.5 %collective-permute-done.7 = bf16[512,128]{1,0:T(8,128)(2,1)S(1)} collective-permute-done((bf16[512,128]{1,0:T(8,128)(2,1)S(1)}, bf16[512,128]{1,0:T(8,128)(2,1)S(1)}, u32[]{:S(2)}, u32[]{:S(2)}) %collective-permute-start.7) | collective-permute-done | bytes 131104 | tf_op jit(solution)/shard_map/ppermute | solution.py:13
  45.1 0.1 add_convert_fusion.1
  45.2 1.6 %collective-permute-start.10 = (bf16[512,128]{1,0:T(8,128)(2,1)S(1)}, bf16[512,128]{1,0:T(8,128)(2,1)S(1)}, u32[]{:S(2)}, u32[]{:S(2)}) collective-permute-start(bf16[512,128]{1,0:T(8,128)(2,1)S(1)} %add_convert_fusion.1), channel_id=1, source_target_pairs={{0,192},{32,224},{64,128},{96,160},{128,64},{160,96},{192,0},{224,... | collective-permute-start | bytes 393224 | tf_op jit(solution)/shard_map/ppermute | solution.py:13
  46.8 1.8 %collective-permute-start.9 = (bf16[512,128]{1,0:T(8,128)(2,1)S(1)}, bf16[512,128]{1,0:T(8,128)(2,1)S(1)}, u32[]{:S(2)}, u32[]{:S(2)}) collective-permute-start(bf16[512,128]{1,0:T(8,128)(2,1)S(1)} %add_convert_fusion.1), channel_id=1, source_target_pairs={{0,64},{32,96},{64,0},{96,32},{128,192},{160,224},{192,128},{224,1... | collective-permute-start | bytes 393224 | tf_op jit(solution)/shard_map/ppermute | solution.py:13
  48.6 0.2 collective-permute-start.8
  48.8 1.5 %collective-permute-done.10 = bf16[512,128]{1,0:T(8,128)(2,1)S(1)} collective-permute-done((bf16[512,128]{1,0:T(8,128)(2,1)S(1)}, bf16[512,128]{1,0:T(8,128)(2,1)S(1)}, u32[]{:S(2)}, u32[]{:S(2)}) %collective-permute-start.10) | collective-permute-done | bytes 131104 | tf_op jit(solution)/shard_map/ppermute | solution.py:13
  50.3 1.5 %collective-permute-done.9 = bf16[512,128]{1,0:T(8,128)(2,1)S(1)} collective-permute-done((bf16[512,128]{1,0:T(8,128)(2,1)S(1)}, bf16[512,128]{1,0:T(8,128)(2,1)S(1)}, u32[]{:S(2)}, u32[]{:S(2)}) %collective-permute-start.9) | collective-permute-done | bytes 131104 | tf_op jit(solution)/shard_map/ppermute | solution.py:13
  51.7 3.3 %collective-permute-done.8 = bf16[512,128]{1,0:T(8,128)(2,1)S(1)} collective-permute-done((bf16[512,128]{1,0:T(8,128)(2,1)S(1)}, bf16[512,128]{1,0:T(8,128)(2,1)S(1)}, u32[]{:S(2)}, u32[]{:S(2)}) %collective-permute-start.8) | collective-permute-done | bytes 131104 | tf_op jit(solution)/shard_map/ppermute | solution.py:13
  55.1 0.1 add_convert_fusion.total_ref
  55.2 1.8 %expand.1 = bf16[2,128,3072]{2,1,0:T(8,128)(2,1)} custom-call(bf16[512,128]{1,0:T(8,128)(2,1)S(1)} %add_convert_fusion.total_ref, bf16[2,256,3072]{2,1,0:T(8,128)(2,1)S(1)} %copy-done.1), custom_call_target="tpu_custom_call" | custom-call | tf_op jit(solution)/shard_map/expand/pallas_call | solution.py:114
  (7 shorter events, 0.0 us)
Async XLA Ops:
  0.0 5.6 %copy-start = (bf16[5,2,256,512]{3,2,1,0:T(8,128)(2,1)S(1)}, bf16[5,2,256,512]{3,2,1,0:T(8,128)(2,1)}, u32[]{:S(2)}) copy-start(bf16[5,2,256,512]{3,2,1,0:T(8,128)(2,1)} %transfer_ref.17) | copy-start | bytes 7864324
  5.5 1.4 %collective-permute-start = (bf16[512,128]{1,0:T(8,128)(2,1)S(1)}, bf16[512,128]{1,0:T(8,128)(2,1)S(1)}, u32[]{:S(2)}, u32[]{:S(2)}) collective-permute-start(bf16[512,128]{1,0:T(8,128)(2,1)S(1)} %leaf.1.coefficients_ref), channel_id=1, source_target_pairs={{0,1},{1,0},{2,3},{3,2},{4,5},{5,4},{6,7},{7,6},{8,9},{9,8},{10,11... | collective-permute-start | bytes 393224 | tf_op jit(solution)/shard_map/ppermute | solution.py:13
  7.2 5.8 %collective-permute-start.1 = (bf16[512,128]{1,0:T(8,128)(2,1)S(1)}, bf16[512,128]{1,0:T(8,128)(2,1)S(1)}, u32[]{:S(2)}, u32[]{:S(2)}) collective-permute-start(bf16[512,128]{1,0:T(8,128)(2,1)S(1)} %partner.4.coefficients_ref), channel_id=1, source_target_pairs={{0,2},{1,3},{2,0},{3,1},{4,6},{5,7},{6,4},{7,5},{8,10},{9,11},{10,... | collective-permute-start | bytes 393224 | tf_op jit(solution)/shard_map/ppermute | solution.py:13
  13.2 9.3 %collective-permute-start.2 = (bf16[512,128]{1,0:T(8,128)(2,1)S(1)}, bf16[512,128]{1,0:T(8,128)(2,1)S(1)}, u32[]{:S(2)}, u32[]{:S(2)}) collective-permute-start(bf16[512,128]{1,0:T(8,128)(2,1)S(1)} %partner.5.coefficients_ref), channel_id=1, source_target_pairs={{0,4},{1,5},{2,6},{3,7},{4,0},{5,1},{6,2},{7,3},{8,12},{9,13},{10,... | collective-permute-start | bytes 393224 | tf_op jit(solution)/shard_map/ppermute | solution.py:13
  16.6 18.8 %collective-permute-start.4 = (bf16[2,256,256]{2,1,0:T(8,128)(2,1)S(1)}, bf16[2,256,256]{2,1,0:T(8,128)(2,1)S(1)}, u32[]{:S(2)}, u32[]{:S(2)}) collective-permute-start(bf16[2,256,256]{2,1,0:T(8,128)(2,1)S(1)} %get-tuple-element.10), channel_id=1, source_target_pairs={{0,16},{1,17},{2,18},{3,19},{4,20},{5,21},{6,22},{7,23},{8,24},{9,... | collective-permute-start | bytes 786440 | tf_op jit(solution)/shard_map/ppermute | solution.py:13
  22.8 12.4 %collective-permute-start.3 = (bf16[512,128]{1,0:T(8,128)(2,1)S(1)}, bf16[512,128]{1,0:T(8,128)(2,1)S(1)}, u32[]{:S(2)}, u32[]{:S(2)}) collective-permute-start(bf16[512,128]{1,0:T(8,128)(2,1)S(1)} %partner.6.coefficients_ref), channel_id=1, source_target_pairs={{0,8},{1,9},{2,10},{3,11},{4,12},{5,13},{6,14},{7,15},{8,0},{9,1},... | collective-permute-start | bytes 393224 | tf_op jit(solution)/shard_map/ppermute | solution.py:13
  35.3 19.8 %copy-start.1 = (bf16[2,256,3072]{2,1,0:T(8,128)(2,1)S(1)}, bf16[2,256,3072]{2,1,0:T(8,128)(2,1)}, u32[]{:S(2)}) copy-start(bf16[2,256,3072]{2,1,0:T(8,128)(2,1)} %basis_ref.1) | copy-start | bytes 9437188
  35.7 6.9 %collective-permute-start.5 = (bf16[512,128]{1,0:T(8,128)(2,1)S(1)}, bf16[512,128]{1,0:T(8,128)(2,1)S(1)}, u32[]{:S(2)}, u32[]{:S(2)}) collective-permute-start(bf16[512,128]{1,0:T(8,128)(2,1)S(1)} %get-tuple-element.11), channel_id=1, source_target_pairs={{0,32},{32,0},{64,96},{96,64},{128,160},{160,128},{192,224},{224,1... | collective-permute-start | bytes 393224 | tf_op jit(solution)/shard_map/ppermute | solution.py:13
  38.9 6.2 %collective-permute-start.7 = (bf16[512,128]{1,0:T(8,128)(2,1)S(1)}, bf16[512,128]{1,0:T(8,128)(2,1)S(1)}, u32[]{:S(2)}, u32[]{:S(2)}) collective-permute-start(bf16[512,128]{1,0:T(8,128)(2,1)S(1)} %get-tuple-element.12), channel_id=1, source_target_pairs={{0,48},{1,49},{2,50},{3,51},{4,52},{5,53},{6,54},{7,55},{8,56},{9,... | collective-permute-start | bytes 393224 | tf_op jit(solution)/shard_map/ppermute | solution.py:13
  40.0 5.1 %collective-permute-start.6 = (bf16[512,128]{1,0:T(8,128)(2,1)S(1)}, bf16[512,128]{1,0:T(8,128)(2,1)S(1)}, u32[]{:S(2)}, u32[]{:S(2)}) collective-permute-start(bf16[512,128]{1,0:T(8,128)(2,1)S(1)} %get-tuple-element.12), channel_id=1, source_target_pairs={{0,16},{1,17},{2,18},{3,19},{4,20},{5,21},{6,22},{7,23},{8,24},{9,... | collective-permute-start | bytes 393224 | tf_op jit(solution)/shard_map/ppermute | solution.py:13
  45.2 5.1 %collective-permute-start.10 = (bf16[512,128]{1,0:T(8,128)(2,1)S(1)}, bf16[512,128]{1,0:T(8,128)(2,1)S(1)}, u32[]{:S(2)}, u32[]{:S(2)}) collective-permute-start(bf16[512,128]{1,0:T(8,128)(2,1)S(1)} %add_convert_fusion.1), channel_id=1, source_target_pairs={{0,192},{32,224},{64,128},{96,160},{128,64},{160,96},{192,0},{224,... | collective-permute-start | bytes 393224 | tf_op jit(solution)/shard_map/ppermute | solution.py:13
  46.8 5.0 %collective-permute-start.9 = (bf16[512,128]{1,0:T(8,128)(2,1)S(1)}, bf16[512,128]{1,0:T(8,128)(2,1)S(1)}, u32[]{:S(2)}, u32[]{:S(2)}) collective-permute-start(bf16[512,128]{1,0:T(8,128)(2,1)S(1)} %add_convert_fusion.1), channel_id=1, source_target_pairs={{0,64},{32,96},{64,0},{96,32},{128,192},{160,224},{192,128},{224,1... | collective-permute-start | bytes 393224 | tf_op jit(solution)/shard_map/ppermute | solution.py:13
  48.6 6.5 %collective-permute-start.8 = (bf16[512,128]{1,0:T(8,128)(2,1)S(1)}, bf16[512,128]{1,0:T(8,128)(2,1)S(1)}, u32[]{:S(2)}, u32[]{:S(2)}) collective-permute-start(bf16[512,128]{1,0:T(8,128)(2,1)S(1)} %add_convert_fusion.1), channel_id=1, source_target_pairs={{0,128},{32,160},{64,192},{96,224},{128,0},{160,32},{192,64},{224,... | collective-permute-start | bytes 393224 | tf_op jit(solution)/shard_map/ppermute | solution.py:13

commit v4 on v3

--- a/solution.py
+++ b/solution.py
@@ -13,36 +13,61 @@
     return lax.ppermute(block, axis, [(place, place ^ mask) for place in range(count)])
 
 
-def leaf_kernel(order_hbm, source_hbm, basis_hbm, out_ref, order_ref, source_ref, basis_ref, by_point_ref, *rest):
-    ordered_refs, (order_done, source_done, basis_done) = rest[:-3], rest[-3:]
+def put(out_ref, parts):
+    rank = out_ref.shape[0] // 2
+    out_ref[:rank] = parts[0].astype(out_ref.dtype)
+    out_ref[rank:] = parts[1].astype(out_ref.dtype)
+
+
+def leaf_kernel(
+    order_hbm, source_hbm, basis_hbm, out_ref, order_ref, row_ref, source_ref, basis_ref,
+    by_point_ref, *rest,
+):
+    ordered_refs, (order_done, row_done, source_done, basis_done) = rest[:-4], rest[-4:]
     _, width, points = source_ref.shape
     rank = basis_ref.shape[1]
     chunk = ordered_refs[0].shape[0] // 2
+    piece = points // (source_done.shape[0] // 2)
     order_copy = pltpu.make_async_copy(order_hbm, order_ref, order_done)
-    source_copies = [
-        pltpu.make_async_copy(source_hbm.at[part], source_ref.at[part], source_done.at[part])
-        for part in range(2)
-    ]
-    basis_copies = [
-        pltpu.make_async_copy(basis_hbm.at[part], basis_ref.at[part], basis_done.at[part])
-        for part in range(2)
-    ]
-    for copy in (order_copy, *source_copies, *basis_copies):
+    row_copy = pltpu.make_async_copy(order_ref, row_ref, row_done)
+    source_copies = []
+    for start in range(0, points, piece):
+        for part in range(2):
+            here = (part, slice(None), pl.ds(start, piece))
+            source_copies.append((
+                part, start,
+                pltpu.make_async_copy(
+                    source_hbm.at[here], source_ref.at[here], source_done.at[len(source_copies)]
+                ),
+            ))
+    basis_copies = []
+    for at in range(len(ordered_refs)):
+        here = (slice(None), slice(None), pl.ds(at * chunk, chunk))
+        basis_copies.append(
+            pltpu.make_async_copy(basis_hbm.at[here], basis_ref.at[here], basis_done.at[at])
+        )
+    order_copy.start()
+    for _, _, copy in source_copies:
         copy.start()
-    for part in range(2):
-        source_copies[part].wait()
-        for start in range(0, points, 256):
+    order_copy.wait()
+    order_ref[...] = 2 * order_ref[...]
+    row_copy.start()
+    for which, (part, first, copy) in enumerate(source_copies):
+        copy.wait()
+        if which == 1:
+            for later in basis_copies:
+                later.start()
+        for start in range(first, first + piece, 256):
             block = source_ref[part, :, start : start + 256].astype(jnp.float32)
             by_point_ref[pl.ds(2 * start + part, 256, stride=2), :] = block.T
-    order_copy.wait()
+    row_copy.wait()
     total = None
     for at in range(len(ordered_refs) + 1):
-        if at == 1:
-            for copy in basis_copies:
-                copy.wait()
+        if at > 0:
+            basis_copies[at - 1].wait()
         if at < len(ordered_refs):
             for row in range(chunk):
-                point = pl.multiple_of(2 * order_ref[0, at * chunk + row], 2)
+                point = pl.multiple_of(row_ref[0, at * chunk + row], 2)
                 ordered_refs[at][2 * row : 2 * row + 2, :] = by_point_ref[pl.ds(point, 2), :]
         if at > 0:
             ordered = jnp.concatenate(
@@ -55,11 +80,13 @@
             basis = basis_ref[:, :, (at - 1) * chunk : at * chunk].reshape(2 * rank, chunk)
             term = jnp.dot(basis, ordered, preferred_element_type=jnp.float32)
             total = term if total is None else total + term
-    out_ref[:rank] = (total[:rank, :width] - total[rank:, width:]).astype(jnp.bfloat16)
-    out_ref[rank:] = (total[:rank, width:] + total[rank:, :width]).astype(jnp.bfloat16)
-
-
-def leaf_coefficients(excitation, point_order, projection, chunk=512):
+    put(
+        out_ref,
+        (total[:rank, :width] - total[rank:, width:], total[:rank, width:] + total[rank:, :width]),
+    )
+
+
+def leaf_coefficients(excitation, point_order, projection, chunk=512, pieces=2):
     _, width, points = excitation.shape
     rank = projection.shape[1]
     point_order, excitation, projection = (
@@ -72,34 +99,40 @@
         out_specs=pl.BlockSpec(memory_space=pltpu.VMEM),
         out_shape=jax.ShapeDtypeStruct((2 * rank, width), jnp.bfloat16),
         scratch_shapes=[
+            pltpu.VMEM((1, points), jnp.int32),
             pltpu.SMEM((1, points), jnp.int32),
             pltpu.VMEM(excitation.shape, jnp.bfloat16),
             pltpu.VMEM(projection.shape, jnp.bfloat16),
             pltpu.VMEM((2 * points, width), jnp.float32),
             *[pltpu.VMEM((2 * chunk, width), jnp.float32)] * (points // chunk),
             pltpu.SemaphoreType.DMA,
-            pltpu.SemaphoreType.DMA((2,)),
-            pltpu.SemaphoreType.DMA((2,)),
+            pltpu.SemaphoreType.DMA,
+            pltpu.SemaphoreType.DMA((2 * pieces,)),
+            pltpu.SemaphoreType.DMA((points // chunk,)),
         ],
         compiler_params=pltpu.CompilerParams(vmem_limit_bytes=24 << 20),
         name="leaf",
     )(point_order, excitation, projection)
 
 
-def expand_kernel(total_ref, basis_ref, out_hbm, left_ref, out_ref, done):
+def expand_kernel(*refs):
+    *term_refs, basis_ref, out_hbm, left_ref, out_ref, done = refs
     rank, points = basis_ref.shape[1:]
-    width = total_ref.shape[1]
+    width = term_refs[0].shape[1]
     chunk = points // done.shape[0]
-    left_ref[:width] = total_ref[:rank].T
-    left_ref[width:] = total_ref[rank:].T
+    total = sum(ref[...].astype(jnp.float32) for ref in term_refs).astype(jnp.bfloat16)
+    real, imag = total[:rank].T, total[rank:].T
+    left_ref[:width, :rank] = real
+    left_ref[:width, rank:] = -imag
+    left_ref[width:, :rank] = imag
+    left_ref[width:, rank:] = real
     left = left_ref[...]
     copies = []
     for at in range(points // chunk):
         here = pl.ds(at * chunk, chunk)
-        by_real = jnp.dot(left, basis_ref[0, :, here], preferred_element_type=jnp.float32)
-        by_imag = jnp.dot(left, basis_ref[1, :, here], preferred_element_type=jnp.float32)
-        out_ref[0, :, here] = (by_real[:width] - by_imag[width:]).astype(jnp.bfloat16)
-        out_ref[1, :, here] = (by_real[width:] + by_imag[:width]).astype(jnp.bfloat16)
+        basis = basis_ref[:, :, here].reshape(2 * rank, chunk)
+        term = jnp.dot(left, basis, preferred_element_type=jnp.float32)
+        out_ref[:, :, here] = term.reshape(2, width, chunk).astype(jnp.bfloat16)
         copies.append(
             pltpu.make_async_copy(out_ref.at[:, :, here], out_hbm.at[:, :, here], done.at[at])
         )
@@ -108,22 +141,22 @@
         copy.wait()
 
 
-def expanded(total, expansion, chunk=512):
+def expanded(terms, expansion, chunk=512):
     _, rank, points = expansion.shape
-    width = total.shape[1]
+    width = terms[0].shape[1]
     return pl.pallas_call(
         expand_kernel,
-        in_specs=[pl.BlockSpec(memory_space=pltpu.VMEM)] * 2,
+        in_specs=[pl.BlockSpec(memory_space=pltpu.VMEM)] * (len(terms) + 1),
         out_specs=pl.BlockSpec(memory_space=pltpu.HBM),
         out_shape=jax.ShapeDtypeStruct((2, width, points), jnp.bfloat16),
         scratch_shapes=[
-            pltpu.VMEM((2 * width, rank), jnp.bfloat16),
+            pltpu.VMEM((2 * width, 2 * rank), jnp.bfloat16),
             pltpu.VMEM((2, width, points), jnp.bfloat16),
             pltpu.SemaphoreType.DMA((points // chunk,)),
         ],
         compiler_params=pltpu.CompilerParams(vmem_limit_bytes=16 << 20),
         name="expand",
-    )(total, expansion)
+    )(*terms, expansion)
 
 
 def half_of(transfer_ref, level, own):
@@ -143,12 +176,6 @@
     return term[:rows, :width] - term[rows:, width:], term[:rows, width:] + term[rows:, :width]
 
 
-def put(out_ref, parts):
-    rank = out_ref.shape[0] // 2
-    out_ref[:rank] = parts[0].astype(out_ref.dtype)
-    out_ref[rank:] = parts[1].astype(out_ref.dtype)
-
-
 def own_kernel(coefficients_ref, transfer_ref, own_ref, *sent_refs, level, sent_level):
     put(own_ref, complex_product(half_of(transfer_ref, level, True), coefficients_ref[...]))
     for sent_ref in sent_refs:
@@ -161,9 +188,17 @@
     put(out_ref, (own_ref[:rank] + real, own_ref[rank:] + imag))
 
 
-def both_kernel(coefficients_ref, foreign_ref, transfer_ref, own_ref, cross_ref, *, level):
-    coefficients = coefficients_ref[...]
-    put(own_ref, complex_product(half_of(transfer_ref, level, True), coefficients))
+def last_kernel(own_term_ref, partner_ref, foreign_ref, transfer_ref, own_ref, cross_ref):
+    levels, _, rank, _ = transfer_ref.shape
+    last = levels - 1
+    real, imag = complex_product(half_of(transfer_ref, last - 1, False), partner_ref[...])
+    coefficients = jnp.concatenate(
+        (
+            (own_term_ref[:rank] + real).astype(jnp.bfloat16),
+            (own_term_ref[rank:] + imag).astype(jnp.bfloat16),
+        )
+    )
+    put(own_ref, complex_product(half_of(transfer_ref, last, True), coefficients))
     put(cross_ref, complex_product(foreign_ref[...], coefficients))
 
 
@@ -196,13 +231,13 @@
         )
         if sent:
             foreign = swap(sent[0], "leaf", 1 << last)
-        coefficients = small_call(
-            functools.partial(partner_kernel, level=level),
-            "partner", node, own_term, partner, transfer,
-        )
+        if level < last - 1:
+            coefficients = small_call(
+                functools.partial(partner_kernel, level=level),
+                "partner", node, own_term, partner, transfer,
+            )
     own, cross = small_call(
-        functools.partial(both_kernel, level=last), "both", [node, node],
-        coefficients, foreign, transfer,
+        last_kernel, "last", [node, node], own_term, partner, foreign, transfer
     )
     leaf_count = lax.axis_size("leaf")
     around = [
@@ -214,12 +249,8 @@
     for term in around:
         total = total + term.astype(jnp.float32)
     total = total.astype(jnp.bfloat16)
-    across = [swap(total, "panel", mask) for mask in (4, 2, 6)]
-    total = total.astype(jnp.float32)
-    for term in across:
-        total = total + term.astype(jnp.float32)
-    total = total.astype(jnp.bfloat16)
-    return expanded(total, expansion)
+    across = [swap(total, "panel", mask) for mask in (2, 4, 6)]
+    return expanded((total, *across), expansion)
 
 
 def solution(mesh):

time: 57 us -> 55.5 us (0.974)
  the two profiles are of different devices: /device:TPU:2 before, /device:TPU:96 now
where the time goes in v4:
time: 55.5 us
  waiting for transfers between devices  30.9 us (56%)
  starting transfers between devices  15.3 us (28%)
  Pallas kernels  9.07 us (16%)
    ppermute x11, waiting for transfers between devices, swap(): lax.ppermute(block, axis, [(place, place ^ mask) for place in range(count)])  30.9 us
    ppermute x11, starting transfers between devices, swap(): lax.ppermute(block, axis, [(place, place ^ mask) for place in range(count)])  15.3 us
    pallas_call x1, Pallas kernels, leaf_coefficients(): pl.pallas_call(leaf_kernel, in_specs=[pl.BlockSpec(memory_space=pltpu.HBM...  5.25 us
    pallas_call x8, Pallas kernels, small_call(): pl.pallas_call(kernel, in_specs=[pl.BlockSpec(memory_space=pltpu.VMEM)] *...  2.03 us
    pallas_call x1, Pallas kernels, expanded(): pl.pallas_call(expand_kernel, in_specs=[pl.BlockSpec(memory_space=pltpu.V...  1.79 us
  transfers between devices with their start and end apart: 11, of which 9 were waited for; matrix products, arithmetic and copies ran while one was open for 0% of the time, Pallas kernels for 2%

profile of v4, /device:TPU:96, one launch (start us, length us, event | category | flops | bytes accessed | tf_op | source)
XLA Modules:
  0.0 55.5 jit_solution(12151240034670594134)
XLA Ops:
  0.0 5.2 %leaf.1.coefficients_ref = bf16[512,128]{1,0:T(8,128)(2,1)S(1)} custom-call(s32[1,3072]{1,0:T(1,128)} %order_hbm.1, bf16[2,128,3072]{2,1,0:T(8,128)(2,1)} %source_hbm.1, bf16[2,256,3072]{2,1,0:T(8,128)(2,1)} %basis_hbm.1), custom_call_target="tpu_custom_call" | custom-call | tf_op jit(solution)/shard_map/leaf/pallas_call | solution.py:96
  5.3 0.1 collective-permute-start
  5.4 0.2 own.4.own_ref
  5.6 1.1 %collective-permute-done.partner_ref = bf16[512,128]{1,0:T(8,128)(2,1)S(1)} collective-permute-done((bf16[512,128]{1,0:T(8,128)(2,1)S(1)}, bf16[512,128]{1,0:T(8,128)(2,1)S(1)}, u32[]{:S(2)}, u32[]{:S(2)}) %collective-permute-start) | collective-permute-done | bytes 131104 | tf_op jit(solution)/shard_map/ppermute | solution.py:13
  6.7 0.2 partner.3.coefficients_ref
  6.9 0.2 collective-permute-start.1
  7.1 0.2 own.5
  7.4 5.2 %collective-permute-done.1.partner_ref = bf16[512,128]{1,0:T(8,128)(2,1)S(1)} collective-permute-done((bf16[512,128]{1,0:T(8,128)(2,1)S(1)}, bf16[512,128]{1,0:T(8,128)(2,1)S(1)}, u32[]{:S(2)}, u32[]{:S(2)}) %collective-permute-start.1) | collective-permute-done | bytes 131104 | tf_op jit(solution)/shard_map/ppermute | solution.py:13
  12.6 0.2 partner.4.coefficients_ref
  12.8 0.1 collective-permute-start.2
  12.9 1.7 %collective-permute-start.4 = (bf16[2,256,256]{2,1,0:T(8,128)(2,1)S(1)}, bf16[2,256,256]{2,1,0:T(8,128)(2,1)S(1)}, u32[]{:S(2)}, u32[]{:S(2)}) collective-permute-start(bf16[2,256,256]{2,1,0:T(8,128)(2,1)S(1)} %get-tuple-element.10), channel_id=1, source_target_pairs={{0,16},{1,17},{2,18},{3,19},{4,20},{5,21},{6,22},{7,23},{8,24},{9,... | collective-permute-start | bytes 786440 | tf_op jit(solution)/shard_map/ppermute | solution.py:13
  14.6 0.2 own.6.own_ref
  14.8 6.4 %collective-permute-done.2.partner_ref = bf16[512,128]{1,0:T(8,128)(2,1)S(1)} collective-permute-done((bf16[512,128]{1,0:T(8,128)(2,1)S(1)}, bf16[512,128]{1,0:T(8,128)(2,1)S(1)}, u32[]{:S(2)}, u32[]{:S(2)}) %collective-permute-start.2) | collective-permute-done | bytes 131104 | tf_op jit(solution)/shard_map/ppermute | solution.py:13
  21.2 0.2 partner.5.coefficients_ref
  21.4 4.7 %collective-permute-start.3 = (bf16[512,128]{1,0:T(8,128)(2,1)S(1)}, bf16[512,128]{1,0:T(8,128)(2,1)S(1)}, u32[]{:S(2)}, u32[]{:S(2)}) collective-permute-start(bf16[512,128]{1,0:T(8,128)(2,1)S(1)} %partner.5.coefficients_ref), channel_id=1, source_target_pairs={{0,8},{1,9},{2,10},{3,11},{4,12},{5,13},{6,14},{7,15},{8,0},{9,1},... | collective-permute-start | bytes 393224 | tf_op jit(solution)/shard_map/ppermute | solution.py:13
  26.1 0.2 own.7.own_term_ref
  26.3 0.0 copy-start.1
  26.3 0.0 collective-permute-done.4.foreign_ref
  26.3 7.3 %collective-permute-done.3.partner_ref = bf16[512,128]{1,0:T(8,128)(2,1)S(1)} collective-permute-done((bf16[512,128]{1,0:T(8,128)(2,1)S(1)}, bf16[512,128]{1,0:T(8,128)(2,1)S(1)}, u32[]{:S(2)}, u32[]{:S(2)}) %collective-permute-start.3) | collective-permute-done | bytes 131104 | tf_op jit(solution)/shard_map/ppermute | solution.py:13
  33.6 0.5 last.1
  34.1 3.3 %collective-permute-start.5 = (bf16[512,128]{1,0:T(8,128)(2,1)S(1)}, bf16[512,128]{1,0:T(8,128)(2,1)S(1)}, u32[]{:S(2)}, u32[]{:S(2)}) collective-permute-start(bf16[512,128]{1,0:T(8,128)(2,1)S(1)} %get-tuple-element.11), channel_id=1, source_target_pairs={{0,32},{32,0},{64,96},{96,64},{128,160},{160,128},{192,224},{224,1... | collective-permute-start | bytes 393224 | tf_op jit(solution)/shard_map/ppermute | solution.py:13
  37.4 1.1 %collective-permute-start.7 = (bf16[512,128]{1,0:T(8,128)(2,1)S(1)}, bf16[512,128]{1,0:T(8,128)(2,1)S(1)}, u32[]{:S(2)}, u32[]{:S(2)}) collective-permute-start(bf16[512,128]{1,0:T(8,128)(2,1)S(1)} %get-tuple-element.12), channel_id=1, source_target_pairs={{0,48},{1,49},{2,50},{3,51},{4,52},{5,53},{6,54},{7,55},{8,56},{9,... | collective-permute-start | bytes 393224 | tf_op jit(solution)/shard_map/ppermute | solution.py:13
  38.4 2.5 %collective-permute-done.5 = bf16[512,128]{1,0:T(8,128)(2,1)S(1)} collective-permute-done((bf16[512,128]{1,0:T(8,128)(2,1)S(1)}, bf16[512,128]{1,0:T(8,128)(2,1)S(1)}, u32[]{:S(2)}, u32[]{:S(2)}) %collective-permute-start.5) | collective-permute-done | bytes 131104 | tf_op jit(solution)/shard_map/ppermute | solution.py:13
  40.9 2.6 %collective-permute-done.7 = bf16[512,128]{1,0:T(8,128)(2,1)S(1)} collective-permute-done((bf16[512,128]{1,0:T(8,128)(2,1)S(1)}, bf16[512,128]{1,0:T(8,128)(2,1)S(1)}, u32[]{:S(2)}, u32[]{:S(2)}) %collective-permute-start.7) | collective-permute-done | bytes 131104 | tf_op jit(solution)/shard_map/ppermute | solution.py:13
  43.6 0.3 collective-permute-done.6
  43.9 0.1 add_convert_fusion.refs_0_
  43.9 2.8 %collective-permute-start.10 = (bf16[512,128]{1,0:T(8,128)(2,1)S(1)}, bf16[512,128]{1,0:T(8,128)(2,1)S(1)}, u32[]{:S(2)}, u32[]{:S(2)}) collective-permute-start(bf16[512,128]{1,0:T(8,128)(2,1)S(1)} %add_convert_fusion.refs_0_), channel_id=1, source_target_pairs={{0,192},{32,224},{64,128},{96,160},{128,64},{160,96},{192,0},{224,... | collective-permute-start | bytes 393224 | tf_op jit(solution)/shard_map/ppermute | solution.py:13
  46.7 0.8 %collective-permute-start.9 = (bf16[512,128]{1,0:T(8,128)(2,1)S(1)}, bf16[512,128]{1,0:T(8,128)(2,1)S(1)}, u32[]{:S(2)}, u32[]{:S(2)}) collective-permute-start(bf16[512,128]{1,0:T(8,128)(2,1)S(1)} %add_convert_fusion.refs_0_), channel_id=1, source_target_pairs={{0,128},{32,160},{64,192},{96,224},{128,0},{160,32},{192,64},{224,... | collective-permute-start | bytes 393224 | tf_op jit(solution)/shard_map/ppermute | solution.py:13
  47.5 0.6 %collective-permute-start.8 = (bf16[512,128]{1,0:T(8,128)(2,1)S(1)}, bf16[512,128]{1,0:T(8,128)(2,1)S(1)}, u32[]{:S(2)}, u32[]{:S(2)}) collective-permute-start(bf16[512,128]{1,0:T(8,128)(2,1)S(1)} %add_convert_fusion.refs_0_), channel_id=1, source_target_pairs={{0,64},{32,96},{64,0},{96,32},{128,192},{160,224},{192,128},{224,1... | collective-permute-start | bytes 393224 | tf_op jit(solution)/shard_map/ppermute | solution.py:13
  48.1 3.5 %collective-permute-done.10.refs_3_ = bf16[512,128]{1,0:T(8,128)(2,1)S(1)} collective-permute-done((bf16[512,128]{1,0:T(8,128)(2,1)S(1)}, bf16[512,128]{1,0:T(8,128)(2,1)S(1)}, u32[]{:S(2)}, u32[]{:S(2)}) %collective-permute-start.10) | collective-permute-done | bytes 131104 | tf_op jit(solution)/shard_map/ppermute | solution.py:13
  51.6 2.1 %collective-permute-done.9.refs_2_ = bf16[512,128]{1,0:T(8,128)(2,1)S(1)} collective-permute-done((bf16[512,128]{1,0:T(8,128)(2,1)S(1)}, bf16[512,128]{1,0:T(8,128)(2,1)S(1)}, u32[]{:S(2)}, u32[]{:S(2)}) %collective-permute-start.9) | collective-permute-done | bytes 131104 | tf_op jit(solution)/shard_map/ppermute | solution.py:13
  53.7 1.8 %expand.1 = bf16[2,128,3072]{2,1,0:T(8,128)(2,1)} custom-call(bf16[512,128]{1,0:T(8,128)(2,1)S(1)} %add_convert_fusion.refs_0_, bf16[512,128]{1,0:T(8,128)(2,1)S(1)} %collective-permute-done.8.refs_1_, bf16[512,128]{1,0:T(8,128)(2,1)S(1)} %collective-permute-done.9.refs_2_, bf16[512,128]{1,0:T(8,128)(2,1)S(1)} %collective-permute-done.10.refs_3_, ...), custom_call_target="tpu_custom_call" | custom-call | tf_op jit(solution)/shard_map/expand/pallas_call | solution.py:147
  (5 shorter events, 0.0 us)
Async XLA Ops:
  0.0 5.4 %copy-start = (bf16[5,2,256,512]{3,2,1,0:T(8,128)(2,1)S(1)}, bf16[5,2,256,512]{3,2,1,0:T(8,128)(2,1)}, u32[]{:S(2)}) copy-start(bf16[5,2,256,512]{3,2,1,0:T(8,128)(2,1)} %transfer_ref.15) | copy-start | bytes 7864324
  5.3 1.4 %collective-permute-start = (bf16[512,128]{1,0:T(8,128)(2,1)S(1)}, bf16[512,128]{1,0:T(8,128)(2,1)S(1)}, u32[]{:S(2)}, u32[]{:S(2)}) collective-permute-start(bf16[512,128]{1,0:T(8,128)(2,1)S(1)} %leaf.1.coefficients_ref), channel_id=1, source_target_pairs={{0,1},{1,0},{2,3},{3,2},{4,5},{5,4},{6,7},{7,6},{8,9},{9,8},{10,11... | collective-permute-start | bytes 393224 | tf_op jit(solution)/shard_map/ppermute | solution.py:13
  6.9 5.6 %collective-permute-start.1 = (bf16[512,128]{1,0:T(8,128)(2,1)S(1)}, bf16[512,128]{1,0:T(8,128)(2,1)S(1)}, u32[]{:S(2)}, u32[]{:S(2)}) collective-permute-start(bf16[512,128]{1,0:T(8,128)(2,1)S(1)} %partner.3.coefficients_ref), channel_id=1, source_target_pairs={{0,2},{1,3},{2,0},{3,1},{4,6},{5,7},{6,4},{7,5},{8,10},{9,11},{10,... | collective-permute-start | bytes 393224 | tf_op jit(solution)/shard_map/ppermute | solution.py:13
  12.8 8.4 %collective-permute-start.2 = (bf16[512,128]{1,0:T(8,128)(2,1)S(1)}, bf16[512,128]{1,0:T(8,128)(2,1)S(1)}, u32[]{:S(2)}, u32[]{:S(2)}) collective-permute-start(bf16[512,128]{1,0:T(8,128)(2,1)S(1)} %partner.4.coefficients_ref), channel_id=1, source_target_pairs={{0,4},{1,5},{2,6},{3,7},{4,0},{5,1},{6,2},{7,3},{8,12},{9,13},{10,... | collective-permute-start | bytes 393224 | tf_op jit(solution)/shard_map/ppermute | solution.py:13
  12.9 13.4 %collective-permute-start.4 = (bf16[2,256,256]{2,1,0:T(8,128)(2,1)S(1)}, bf16[2,256,256]{2,1,0:T(8,128)(2,1)S(1)}, u32[]{:S(2)}, u32[]{:S(2)}) collective-permute-start(bf16[2,256,256]{2,1,0:T(8,128)(2,1)S(1)} %get-tuple-element.10), channel_id=1, source_target_pairs={{0,16},{1,17},{2,18},{3,19},{4,20},{5,21},{6,22},{7,23},{8,24},{9,... | collective-permute-start | bytes 786440 | tf_op jit(solution)/shard_map/ppermute | solution.py:13
  21.4 12.2 %collective-permute-start.3 = (bf16[512,128]{1,0:T(8,128)(2,1)S(1)}, bf16[512,128]{1,0:T(8,128)(2,1)S(1)}, u32[]{:S(2)}, u32[]{:S(2)}) collective-permute-start(bf16[512,128]{1,0:T(8,128)(2,1)S(1)} %partner.5.coefficients_ref), channel_id=1, source_target_pairs={{0,8},{1,9},{2,10},{3,11},{4,12},{5,13},{6,14},{7,15},{8,0},{9,1},... | collective-permute-start | bytes 393224 | tf_op jit(solution)/shard_map/ppermute | solution.py:13
  26.3 27.4 %copy-start.1 = (bf16[2,256,3072]{2,1,0:T(8,128)(2,1)S(1)}, bf16[2,256,3072]{2,1,0:T(8,128)(2,1)}, u32[]{:S(2)}) copy-start(bf16[2,256,3072]{2,1,0:T(8,128)(2,1)} %refs_4_.1) | copy-start | bytes 9437188
  34.1 6.8 %collective-permute-start.5 = (bf16[512,128]{1,0:T(8,128)(2,1)S(1)}, bf16[512,128]{1,0:T(8,128)(2,1)S(1)}, u32[]{:S(2)}, u32[]{:S(2)}) collective-permute-start(bf16[512,128]{1,0:T(8,128)(2,1)S(1)} %get-tuple-element.11), channel_id=1, source_target_pairs={{0,32},{32,0},{64,96},{96,64},{128,160},{160,128},{192,224},{224,1... | collective-permute-start | bytes 393224 | tf_op jit(solution)/shard_map/ppermute | solution.py:13
  37.4 6.2 %collective-permute-start.7 = (bf16[512,128]{1,0:T(8,128)(2,1)S(1)}, bf16[512,128]{1,0:T(8,128)(2,1)S(1)}, u32[]{:S(2)}, u32[]{:S(2)}) collective-permute-start(bf16[512,128]{1,0:T(8,128)(2,1)S(1)} %get-tuple-element.12), channel_id=1, source_target_pairs={{0,48},{1,49},{2,50},{3,51},{4,52},{5,53},{6,54},{7,55},{8,56},{9,... | collective-permute-start | bytes 393224 | tf_op jit(solution)/shard_map/ppermute | solution.py:13
  38.4 5.4 %collective-permute-start.6 = (bf16[512,128]{1,0:T(8,128)(2,1)S(1)}, bf16[512,128]{1,0:T(8,128)(2,1)S(1)}, u32[]{:S(2)}, u32[]{:S(2)}) collective-permute-start(bf16[512,128]{1,0:T(8,128)(2,1)S(1)} %get-tuple-element.12), channel_id=1, source_target_pairs={{0,16},{1,17},{2,18},{3,19},{4,20},{5,21},{6,22},{7,23},{8,24},{9,... | collective-permute-start | bytes 393224 | tf_op jit(solution)/shard_map/ppermute | solution.py:13
  43.9 7.7 %collective-permute-start.10 = (bf16[512,128]{1,0:T(8,128)(2,1)S(1)}, bf16[512,128]{1,0:T(8,128)(2,1)S(1)}, u32[]{:S(2)}, u32[]{:S(2)}) collective-permute-start(bf16[512,128]{1,0:T(8,128)(2,1)S(1)} %add_convert_fusion.refs_0_), channel_id=1, source_target_pairs={{0,192},{32,224},{64,128},{96,160},{128,64},{160,96},{192,0},{224,... | collective-permute-start | bytes 393224 | tf_op jit(solution)/shard_map/ppermute | solution.py:13
  46.7 6.9 %collective-permute-start.9 = (bf16[512,128]{1,0:T(8,128)(2,1)S(1)}, bf16[512,128]{1,0:T(8,128)(2,1)S(1)}, u32[]{:S(2)}, u32[]{:S(2)}) collective-permute-start(bf16[512,128]{1,0:T(8,128)(2,1)S(1)} %add_convert_fusion.refs_0_), channel_id=1, source_target_pairs={{0,128},{32,160},{64,192},{96,224},{128,0},{160,32},{192,64},{224,... | collective-permute-start | bytes 393224 | tf_op jit(solution)/shard_map/ppermute | solution.py:13
  47.5 6.1 %collective-permute-start.8 = (bf16[512,128]{1,0:T(8,128)(2,1)S(1)}, bf16[512,128]{1,0:T(8,128)(2,1)S(1)}, u32[]{:S(2)}, u32[]{:S(2)}) collective-permute-start(bf16[512,128]{1,0:T(8,128)(2,1)S(1)} %add_convert_fusion.refs_0_), channel_id=1, source_target_pairs={{0,64},{32,96},{64,0},{96,32},{128,192},{160,224},{192,128},{224,1... | collective-permute-start | bytes 393224 | tf_op jit(solution)/shard_map/ppermute | solution.py:13

commit v5 on v4

--- a/solution.py
+++ b/solution.py
@@ -20,10 +20,11 @@
 
 
 def leaf_kernel(
-    order_hbm, source_hbm, basis_hbm, out_ref, order_ref, row_ref, source_ref, basis_ref,
-    by_point_ref, *rest,
+    order_hbm, source_hbm, basis_hbm, transfer_hbm, out_ref, transfer_ref, order_ref, row_ref,
+    source_ref, basis_ref, by_point_ref, *rest,
 ):
-    ordered_refs, (order_done, row_done, source_done, basis_done) = rest[:-4], rest[-4:]
+    ordered_refs, rest = rest[:-5], rest[-5:]
+    order_done, row_done, source_done, basis_done, transfer_done = rest
     _, width, points = source_ref.shape
     rank = basis_ref.shape[1]
     chunk = ordered_refs[0].shape[0] // 2
@@ -46,21 +47,24 @@
         basis_copies.append(
             pltpu.make_async_copy(basis_hbm.at[here], basis_ref.at[here], basis_done.at[at])
         )
+    transfer_copy = pltpu.make_async_copy(transfer_hbm, transfer_ref, transfer_done)
     order_copy.start()
     for _, _, copy in source_copies:
         copy.start()
+    for copy in basis_copies[:1]:
+        copy.start()
     order_copy.wait()
+    for copy in basis_copies[1:]:
+        copy.start()
     order_ref[...] = 2 * order_ref[...]
     row_copy.start()
-    for which, (part, first, copy) in enumerate(source_copies):
+    for part, first, copy in source_copies:
         copy.wait()
-        if which == 1:
-            for later in basis_copies:
-                later.start()
         for start in range(first, first + piece, 256):
             block = source_ref[part, :, start : start + 256].astype(jnp.float32)
             by_point_ref[pl.ds(2 * start + part, 256, stride=2), :] = block.T
     row_copy.wait()
+    transfer_copy.start()
     total = None
     for at in range(len(ordered_refs) + 1):
         if at > 0:
@@ -80,24 +84,28 @@
             basis = basis_ref[:, :, (at - 1) * chunk : at * chunk].reshape(2 * rank, chunk)
             term = jnp.dot(basis, ordered, preferred_element_type=jnp.float32)
             total = term if total is None else total + term
+    transfer_copy.wait()
     put(
         out_ref,
         (total[:rank, :width] - total[rank:, width:], total[:rank, width:] + total[rank:, :width]),
     )
 
 
-def leaf_coefficients(excitation, point_order, projection, chunk=512, pieces=2):
+def leaf_coefficients(excitation, point_order, projection, transfer, chunk=512, pieces=1):
     _, width, points = excitation.shape
     rank = projection.shape[1]
-    point_order, excitation, projection = (
+    operands = [
         pltpu.with_memory_space_constraint(array, pltpu.HBM)
-        for array in (point_order, excitation, projection)
-    )
+        for array in (point_order, excitation, projection, transfer)
+    ]
     return pl.pallas_call(
         leaf_kernel,
-        in_specs=[pl.BlockSpec(memory_space=pltpu.HBM)] * 3,
-        out_specs=pl.BlockSpec(memory_space=pltpu.VMEM),
-        out_shape=jax.ShapeDtypeStruct((2 * rank, width), jnp.bfloat16),
+        in_specs=[pl.BlockSpec(memory_space=pltpu.HBM)] * len(operands),
+        out_specs=[pl.BlockSpec(memory_space=pltpu.VMEM)] * 2,
+        out_shape=[
+            jax.ShapeDtypeStruct((2 * rank, width), jnp.bfloat16),
+            jax.ShapeDtypeStruct(transfer.shape, jnp.bfloat16),
+        ],
         scratch_shapes=[
             pltpu.VMEM((1, points), jnp.int32),
             pltpu.SMEM((1, points), jnp.int32),
@@ -109,10 +117,11 @@
             pltpu.SemaphoreType.DMA,
             pltpu.SemaphoreType.DMA((2 * pieces,)),
             pltpu.SemaphoreType.DMA((points // chunk,)),
+            pltpu.SemaphoreType.DMA,
         ],
         compiler_params=pltpu.CompilerParams(vmem_limit_bytes=24 << 20),
         name="leaf",
-    )(point_order, excitation, projection)
+    )(*operands)
 
 
 def expand_kernel(*refs):
@@ -215,7 +224,7 @@
 
 
 def per_device(excitation, point_order, projection, transfer, expansion):
-    coefficients = leaf_coefficients(excitation, point_order, projection)
+    coefficients, transfer = leaf_coefficients(excitation, point_order, projection, transfer)
     levels, _, rank, _ = transfer.shape
     last = levels - 1
     shape = coefficients.shape

time: 55.5 us -> 55.1 us (level)
  no operation moved by 1% of the time
where the time goes in v5:
time: 55.1 us; the launch traced here: 55 us
  waiting for transfers between devices  30.9 us (56%)
  starting transfers between devices  15.3 us (28%)
  Pallas kernels  8.62 us (16%)
    ppermute x11, waiting for transfers between devices, swap(): lax.ppermute(block, axis, [(place, place ^ mask) for place in range(count)])  30.9 us
    ppermute x11, starting transfers between devices, swap(): lax.ppermute(block, axis, [(place, place ^ mask) for place in range(count)])  15.3 us
    pallas_call x1, Pallas kernels, leaf_coefficients(): pl.pallas_call(leaf_kernel, in_specs=[pl.BlockSpec(memory_space=pltpu.HBM...  4.8 us
    pallas_call x8, Pallas kernels, small_call(): pl.pallas_call(kernel, in_specs=[pl.BlockSpec(memory_space=pltpu.VMEM)] *...  2.03 us
    pallas_call x1, Pallas kernels, expanded(): pl.pallas_call(expand_kernel, in_specs=[pl.BlockSpec(memory_space=pltpu.V...  1.79 us
  transfers between devices with their start and end apart: 11, of which 9 were waited for; matrix products, arithmetic and copies ran while one was open for 0% of the time, Pallas kernels for 2%

profile of v5, /device:TPU:96, one launch (start us, length us, event | category | flops | bytes accessed | tf_op | source)
XLA Modules:
  0.0 55.0 jit_solution(4307571267159208097)
XLA Ops:
  0.0 4.8 %leaf.1 = (bf16[512,128]{1,0:T(8,128)(2,1)S(1)}, bf16[5,2,256,512]{3,2,1,0:T(8,128)(2,1)S(1)}) custom-call(s32[1,3072]{1,0:T(1,128)} %order_hbm.1, bf16[2,128,3072]{2,1,0:T(8,128)(2,1)} %source_hbm.1, bf16[2,256,3072]{2,1,0:T(8,128)(2,1)} %basis_hbm.1, bf16[5,2,256,512]{3,2,1,0:T(8,128)(2,1)} %transfer_hbm.1), custom_call_target="tpu_custom_call" | custom-call | tf_op jit(solution)/shard_map/leaf/pallas_call | solution.py:101
  4.8 0.1 collective-permute-start
  4.9 0.2 own.4.own_ref
  5.1 1.1 %collective-permute-done.partner_ref = bf16[512,128]{1,0:T(8,128)(2,1)S(1)} collective-permute-done((bf16[512,128]{1,0:T(8,128)(2,1)S(1)}, bf16[512,128]{1,0:T(8,128)(2,1)S(1)}, u32[]{:S(2)}, u32[]{:S(2)}) %collective-permute-start) | collective-permute-done | bytes 131104 | tf_op jit(solution)/shard_map/ppermute | solution.py:13
  6.2 0.2 partner.3.coefficients_ref
  6.5 0.2 collective-permute-start.1
  6.7 0.2 own.5
  6.9 5.2 %collective-permute-done.1.partner_ref = bf16[512,128]{1,0:T(8,128)(2,1)S(1)} collective-permute-done((bf16[512,128]{1,0:T(8,128)(2,1)S(1)}, bf16[512,128]{1,0:T(8,128)(2,1)S(1)}, u32[]{:S(2)}, u32[]{:S(2)}) %collective-permute-start.1) | collective-permute-done | bytes 131104 | tf_op jit(solution)/shard_map/ppermute | solution.py:13
  12.1 0.2 partner.4.coefficients_ref
  12.3 0.1 collective-permute-start.2
  12.4 1.7 %collective-permute-start.4 = (bf16[2,256,256]{2,1,0:T(8,128)(2,1)S(1)}, bf16[2,256,256]{2,1,0:T(8,128)(2,1)S(1)}, u32[]{:S(2)}, u32[]{:S(2)}) collective-permute-start(bf16[2,256,256]{2,1,0:T(8,128)(2,1)S(1)} %get-tuple-element.14), channel_id=1, source_target_pairs={{0,16},{1,17},{2,18},{3,19},{4,20},{5,21},{6,22},{7,23},{8,24},{9,... | collective-permute-start | bytes 786440 | tf_op jit(solution)/shard_map/ppermute | solution.py:13
  14.1 0.2 own.6.own_ref
  14.3 6.4 %collective-permute-done.2.partner_ref = bf16[512,128]{1,0:T(8,128)(2,1)S(1)} collective-permute-done((bf16[512,128]{1,0:T(8,128)(2,1)S(1)}, bf16[512,128]{1,0:T(8,128)(2,1)S(1)}, u32[]{:S(2)}, u32[]{:S(2)}) %collective-permute-start.2) | collective-permute-done | bytes 131104 | tf_op jit(solution)/shard_map/ppermute | solution.py:13
  20.7 0.2 partner.5.coefficients_ref
  20.9 4.7 %collective-permute-start.3 = (bf16[512,128]{1,0:T(8,128)(2,1)S(1)}, bf16[512,128]{1,0:T(8,128)(2,1)S(1)}, u32[]{:S(2)}, u32[]{:S(2)}) collective-permute-start(bf16[512,128]{1,0:T(8,128)(2,1)S(1)} %partner.5.coefficients_ref), channel_id=1, source_target_pairs={{0,8},{1,9},{2,10},{3,11},{4,12},{5,13},{6,14},{7,15},{8,0},{9,1},... | collective-permute-start | bytes 393224 | tf_op jit(solution)/shard_map/ppermute | solution.py:13
  25.6 0.2 own.7.own_term_ref
  25.9 0.0 copy-start
  25.9 0.0 collective-permute-done.4.foreign_ref
  25.9 7.3 %collective-permute-done.3.partner_ref = bf16[512,128]{1,0:T(8,128)(2,1)S(1)} collective-permute-done((bf16[512,128]{1,0:T(8,128)(2,1)S(1)}, bf16[512,128]{1,0:T(8,128)(2,1)S(1)}, u32[]{:S(2)}, u32[]{:S(2)}) %collective-permute-start.3) | collective-permute-done | bytes 131104 | tf_op jit(solution)/shard_map/ppermute | solution.py:13
  33.2 0.5 last.1
  33.7 3.3 %collective-permute-start.5 = (bf16[512,128]{1,0:T(8,128)(2,1)S(1)}, bf16[512,128]{1,0:T(8,128)(2,1)S(1)}, u32[]{:S(2)}, u32[]{:S(2)}) collective-permute-start(bf16[512,128]{1,0:T(8,128)(2,1)S(1)} %get-tuple-element.15), channel_id=1, source_target_pairs={{0,32},{32,0},{64,96},{96,64},{128,160},{160,128},{192,224},{224,1... | collective-permute-start | bytes 393224 | tf_op jit(solution)/shard_map/ppermute | solution.py:13
  37.0 1.1 %collective-permute-start.7 = (bf16[512,128]{1,0:T(8,128)(2,1)S(1)}, bf16[512,128]{1,0:T(8,128)(2,1)S(1)}, u32[]{:S(2)}, u32[]{:S(2)}) collective-permute-start(bf16[512,128]{1,0:T(8,128)(2,1)S(1)} %get-tuple-element.16), channel_id=1, source_target_pairs={{0,48},{1,49},{2,50},{3,51},{4,52},{5,53},{6,54},{7,55},{8,56},{9,... | collective-permute-start | bytes 393224 | tf_op jit(solution)/shard_map/ppermute | solution.py:13
  38.0 2.6 %collective-permute-done.5 = bf16[512,128]{1,0:T(8,128)(2,1)S(1)} collective-permute-done((bf16[512,128]{1,0:T(8,128)(2,1)S(1)}, bf16[512,128]{1,0:T(8,128)(2,1)S(1)}, u32[]{:S(2)}, u32[]{:S(2)}) %collective-permute-start.5) | collective-permute-done | bytes 131104 | tf_op jit(solution)/shard_map/ppermute | solution.py:13
  40.6 2.5 %collective-permute-done.7 = bf16[512,128]{1,0:T(8,128)(2,1)S(1)} collective-permute-done((bf16[512,128]{1,0:T(8,128)(2,1)S(1)}, bf16[512,128]{1,0:T(8,128)(2,1)S(1)}, u32[]{:S(2)}, u32[]{:S(2)}) %collective-permute-start.7) | collective-permute-done | bytes 131104 | tf_op jit(solution)/shard_map/ppermute | solution.py:13
  43.1 0.2 collective-permute-done.6
  43.3 0.1 add_convert_fusion.refs_0_
  43.4 2.9 %collective-permute-start.10 = (bf16[512,128]{1,0:T(8,128)(2,1)S(1)}, bf16[512,128]{1,0:T(8,128)(2,1)S(1)}, u32[]{:S(2)}, u32[]{:S(2)}) collective-permute-start(bf16[512,128]{1,0:T(8,128)(2,1)S(1)} %add_convert_fusion.refs_0_), channel_id=1, source_target_pairs={{0,192},{32,224},{64,128},{96,160},{128,64},{160,96},{192,0},{224,... | collective-permute-start | bytes 393224 | tf_op jit(solution)/shard_map/ppermute | solution.py:13
  46.3 0.8 %collective-permute-start.9 = (bf16[512,128]{1,0:T(8,128)(2,1)S(1)}, bf16[512,128]{1,0:T(8,128)(2,1)S(1)}, u32[]{:S(2)}, u32[]{:S(2)}) collective-permute-start(bf16[512,128]{1,0:T(8,128)(2,1)S(1)} %add_convert_fusion.refs_0_), channel_id=1, source_target_pairs={{0,128},{32,160},{64,192},{96,224},{128,0},{160,32},{192,64},{224,... | collective-permute-start | bytes 393224 | tf_op jit(solution)/shard_map/ppermute | solution.py:13
  47.1 0.5 collective-permute-start.8
  47.6 3.5 %collective-permute-done.10.refs_3_ = bf16[512,128]{1,0:T(8,128)(2,1)S(1)} collective-permute-done((bf16[512,128]{1,0:T(8,128)(2,1)S(1)}, bf16[512,128]{1,0:T(8,128)(2,1)S(1)}, u32[]{:S(2)}, u32[]{:S(2)}) %collective-permute-start.10) | collective-permute-done | bytes 131104 | tf_op jit(solution)/shard_map/ppermute | solution.py:13
  51.1 2.1 %collective-permute-done.9.refs_2_ = bf16[512,128]{1,0:T(8,128)(2,1)S(1)} collective-permute-done((bf16[512,128]{1,0:T(8,128)(2,1)S(1)}, bf16[512,128]{1,0:T(8,128)(2,1)S(1)}, u32[]{:S(2)}, u32[]{:S(2)}) %collective-permute-start.9) | collective-permute-done | bytes 131104 | tf_op jit(solution)/shard_map/ppermute | solution.py:13
  53.2 1.8 %expand.1 = bf16[2,128,3072]{2,1,0:T(8,128)(2,1)} custom-call(bf16[512,128]{1,0:T(8,128)(2,1)S(1)} %add_convert_fusion.refs_0_, bf16[512,128]{1,0:T(8,128)(2,1)S(1)} %collective-permute-done.8.refs_1_, bf16[512,128]{1,0:T(8,128)(2,1)S(1)} %collective-permute-done.9.refs_2_, bf16[512,128]{1,0:T(8,128)(2,1)S(1)} %collective-permute-done.10.refs_3_, ...), custom_call_target="tpu_custom_call" | custom-call | tf_op jit(solution)/shard_map/expand/pallas_call | solution.py:156
  (3 shorter events, 0.0 us)
Async XLA Ops:
  4.8 1.4 %collective-permute-start = (bf16[512,128]{1,0:T(8,128)(2,1)S(1)}, bf16[512,128]{1,0:T(8,128)(2,1)S(1)}, u32[]{:S(2)}, u32[]{:S(2)}) collective-permute-start(bf16[512,128]{1,0:T(8,128)(2,1)S(1)} %get-tuple-element.11.coefficients_ref), channel_id=1, source_target_pairs={{0,1},{1,0},{2,3},{3,2},{4,5},{5,4},{6,7},{7,6},{8,9},{9,8},{10,11... | collective-permute-start | bytes 393224 | tf_op jit(solution)/shard_map/ppermute | solution.py:13
  6.5 5.6 %collective-permute-start.1 = (bf16[512,128]{1,0:T(8,128)(2,1)S(1)}, bf16[512,128]{1,0:T(8,128)(2,1)S(1)}, u32[]{:S(2)}, u32[]{:S(2)}) collective-permute-start(bf16[512,128]{1,0:T(8,128)(2,1)S(1)} %partner.3.coefficients_ref), channel_id=1, source_target_pairs={{0,2},{1,3},{2,0},{3,1},{4,6},{5,7},{6,4},{7,5},{8,10},{9,11},{10,... | collective-permute-start | bytes 393224 | tf_op jit(solution)/shard_map/ppermute | solution.py:13
  12.3 8.4 %collective-permute-start.2 = (bf16[512,128]{1,0:T(8,128)(2,1)S(1)}, bf16[512,128]{1,0:T(8,128)(2,1)S(1)}, u32[]{:S(2)}, u32[]{:S(2)}) collective-permute-start(bf16[512,128]{1,0:T(8,128)(2,1)S(1)} %partner.4.coefficients_ref), channel_id=1, source_target_pairs={{0,4},{1,5},{2,6},{3,7},{4,0},{5,1},{6,2},{7,3},{8,12},{9,13},{10,... | collective-permute-start | bytes 393224 | tf_op jit(solution)/shard_map/ppermute | solution.py:13
  12.4 13.5 %collective-permute-start.4 = (bf16[2,256,256]{2,1,0:T(8,128)(2,1)S(1)}, bf16[2,256,256]{2,1,0:T(8,128)(2,1)S(1)}, u32[]{:S(2)}, u32[]{:S(2)}) collective-permute-start(bf16[2,256,256]{2,1,0:T(8,128)(2,1)S(1)} %get-tuple-element.14), channel_id=1, source_target_pairs={{0,16},{1,17},{2,18},{3,19},{4,20},{5,21},{6,22},{7,23},{8,24},{9,... | collective-permute-start | bytes 786440 | tf_op jit(solution)/shard_map/ppermute | solution.py:13
  20.9 12.2 %collective-permute-start.3 = (bf16[512,128]{1,0:T(8,128)(2,1)S(1)}, bf16[512,128]{1,0:T(8,128)(2,1)S(1)}, u32[]{:S(2)}, u32[]{:S(2)}) collective-permute-start(bf16[512,128]{1,0:T(8,128)(2,1)S(1)} %partner.5.coefficients_ref), channel_id=1, source_target_pairs={{0,8},{1,9},{2,10},{3,11},{4,12},{5,13},{6,14},{7,15},{8,0},{9,1},... | collective-permute-start | bytes 393224 | tf_op jit(solution)/shard_map/ppermute | solution.py:13
  25.9 27.3 %copy-start = (bf16[2,256,3072]{2,1,0:T(8,128)(2,1)S(1)}, bf16[2,256,3072]{2,1,0:T(8,128)(2,1)}, u32[]{:S(2)}) copy-start(bf16[2,256,3072]{2,1,0:T(8,128)(2,1)} %refs_4_.1) | copy-start | bytes 9437188
  33.7 7.0 %collective-permute-start.5 = (bf16[512,128]{1,0:T(8,128)(2,1)S(1)}, bf16[512,128]{1,0:T(8,128)(2,1)S(1)}, u32[]{:S(2)}, u32[]{:S(2)}) collective-permute-start(bf16[512,128]{1,0:T(8,128)(2,1)S(1)} %get-tuple-element.15), channel_id=1, source_target_pairs={{0,32},{32,0},{64,96},{96,64},{128,160},{160,128},{192,224},{224,1... | collective-permute-start | bytes 393224 | tf_op jit(solution)/shard_map/ppermute | solution.py:13
  37.0 6.2 %collective-permute-start.7 = (bf16[512,128]{1,0:T(8,128)(2,1)S(1)}, bf16[512,128]{1,0:T(8,128)(2,1)S(1)}, u32[]{:S(2)}, u32[]{:S(2)}) collective-permute-start(bf16[512,128]{1,0:T(8,128)(2,1)S(1)} %get-tuple-element.16), channel_id=1, source_target_pairs={{0,48},{1,49},{2,50},{3,51},{4,52},{5,53},{6,54},{7,55},{8,56},{9,... | collective-permute-start | bytes 393224 | tf_op jit(solution)/shard_map/ppermute | solution.py:13
  38.0 5.3 %collective-permute-start.6 = (bf16[512,128]{1,0:T(8,128)(2,1)S(1)}, bf16[512,128]{1,0:T(8,128)(2,1)S(1)}, u32[]{:S(2)}, u32[]{:S(2)}) collective-permute-start(bf16[512,128]{1,0:T(8,128)(2,1)S(1)} %get-tuple-element.16), channel_id=1, source_target_pairs={{0,16},{1,17},{2,18},{3,19},{4,20},{5,21},{6,22},{7,23},{8,24},{9,... | collective-permute-start | bytes 393224 | tf_op jit(solution)/shard_map/ppermute | solution.py:13
  43.4 7.7 %collective-permute-start.10 = (bf16[512,128]{1,0:T(8,128)(2,1)S(1)}, bf16[512,128]{1,0:T(8,128)(2,1)S(1)}, u32[]{:S(2)}, u32[]{:S(2)}) collective-permute-start(bf16[512,128]{1,0:T(8,128)(2,1)S(1)} %add_convert_fusion.refs_0_), channel_id=1, source_target_pairs={{0,192},{32,224},{64,128},{96,160},{128,64},{160,96},{192,0},{224,... | collective-permute-start | bytes 393224 | tf_op jit(solution)/shard_map/ppermute | solution.py:13
  46.3 6.9 %collective-permute-start.9 = (bf16[512,128]{1,0:T(8,128)(2,1)S(1)}, bf16[512,128]{1,0:T(8,128)(2,1)S(1)}, u32[]{:S(2)}, u32[]{:S(2)}) collective-permute-start(bf16[512,128]{1,0:T(8,128)(2,1)S(1)} %add_convert_fusion.refs_0_), channel_id=1, source_target_pairs={{0,128},{32,160},{64,192},{96,224},{128,0},{160,32},{192,64},{224,... | collective-permute-start | bytes 393224 | tf_op jit(solution)/shard_map/ppermute | solution.py:13
  47.1 6.1 %collective-permute-start.8 = (bf16[512,128]{1,0:T(8,128)(2,1)S(1)}, bf16[512,128]{1,0:T(8,128)(2,1)S(1)}, u32[]{:S(2)}, u32[]{:S(2)}) collective-permute-start(bf16[512,128]{1,0:T(8,128)(2,1)S(1)} %add_convert_fusion.refs_0_), channel_id=1, source_target_pairs={{0,64},{32,96},{64,0},{96,32},{128,192},{160,224},{192,128},{224,1... | collective-permute-start | bytes 393224 | tf_op jit(solution)/shard_map/ppermute | solution.py:13

commit v6 on v5

--- a/solution.py
+++ b/solution.py
@@ -150,7 +150,7 @@
         copy.wait()
 
 
-def expanded(terms, expansion, chunk=512):
+def expanded(terms, expansion, chunk=256):
     _, rank, points = expansion.shape
     width = terms[0].shape[1]
     return pl.pallas_call(

time: 55.1 us -> 55.3 us (level)
  no operation moved by 1% of the time
where the time goes in v6:
time: 55.3 us; the launch traced here: 55.2 us
  waiting for transfers between devices  30.9 us (56%)
  starting transfers between devices  15.3 us (28%)
  Pallas kernels  8.82 us (16%)
    ppermute x11, waiting for transfers between devices, swap(): lax.ppermute(block, axis, [(place, place ^ mask) for place in range(count)])  30.9 us
    ppermute x11, starting transfers between devices, swap(): lax.ppermute(block, axis, [(place, place ^ mask) for place in range(count)])  15.3 us
    pallas_call x1, Pallas kernels, leaf_coefficients(): pl.pallas_call(leaf_kernel, in_specs=[pl.BlockSpec(memory_space=pltpu.HBM...  4.8 us
    pallas_call x8, Pallas kernels, small_call(): pl.pallas_call(kernel, in_specs=[pl.BlockSpec(memory_space=pltpu.VMEM)] *...  2.05 us
    pallas_call x1, Pallas kernels, expanded(): pl.pallas_call(expand_kernel, in_specs=[pl.BlockSpec(memory_space=pltpu.V...  1.98 us
  transfers between devices with their start and end apart: 11, of which 9 were waited for; matrix products, arithmetic and copies ran while one was open for 0% of the time, Pallas kernels for 2%

profile of v6, /device:TPU:96, one launch (start us, length us, event | category | flops | bytes accessed | tf_op | source)
XLA Modules:
  0.0 55.2 jit_solution(16069818947880176164)
XLA Ops:
  0.0 4.8 %leaf.1 = (bf16[512,128]{1,0:T(8,128)(2,1)S(1)}, bf16[5,2,256,512]{3,2,1,0:T(8,128)(2,1)S(1)}) custom-call(s32[1,3072]{1,0:T(1,128)} %order_hbm.1, bf16[2,128,3072]{2,1,0:T(8,128)(2,1)} %source_hbm.1, bf16[2,256,3072]{2,1,0:T(8,128)(2,1)} %basis_hbm.1, bf16[5,2,256,512]{3,2,1,0:T(8,128)(2,1)} %transfer_hbm.1), custom_call_target="tpu_custom_call" | custom-call | tf_op jit(solution)/shard_map/leaf/pallas_call | solution.py:101
  4.8 0.1 collective-permute-start
  4.9 0.2 own.4.own_ref
  5.1 1.1 %collective-permute-done.partner_ref = bf16[512,128]{1,0:T(8,128)(2,1)S(1)} collective-permute-done((bf16[512,128]{1,0:T(8,128)(2,1)S(1)}, bf16[512,128]{1,0:T(8,128)(2,1)S(1)}, u32[]{:S(2)}, u32[]{:S(2)}) %collective-permute-start) | collective-permute-done | bytes 131104 | tf_op jit(solution)/shard_map/ppermute | solution.py:13
  6.2 0.2 partner.3.coefficients_ref
  6.5 0.2 collective-permute-start.1
  6.7 0.2 own.5
  6.9 5.2 %collective-permute-done.1.partner_ref = bf16[512,128]{1,0:T(8,128)(2,1)S(1)} collective-permute-done((bf16[512,128]{1,0:T(8,128)(2,1)S(1)}, bf16[512,128]{1,0:T(8,128)(2,1)S(1)}, u32[]{:S(2)}, u32[]{:S(2)}) %collective-permute-start.1) | collective-permute-done | bytes 131104 | tf_op jit(solution)/shard_map/ppermute | solution.py:13
  12.1 0.2 partner.4.coefficients_ref
  12.3 0.1 collective-permute-start.2
  12.4 1.7 %collective-permute-start.4 = (bf16[2,256,256]{2,1,0:T(8,128)(2,1)S(1)}, bf16[2,256,256]{2,1,0:T(8,128)(2,1)S(1)}, u32[]{:S(2)}, u32[]{:S(2)}) collective-permute-start(bf16[2,256,256]{2,1,0:T(8,128)(2,1)S(1)} %get-tuple-element.14), channel_id=1, source_target_pairs={{0,16},{1,17},{2,18},{3,19},{4,20},{5,21},{6,22},{7,23},{8,24},{9,... | collective-permute-start | bytes 786440 | tf_op jit(solution)/shard_map/ppermute | solution.py:13
  14.1 0.2 own.6.own_ref
  14.3 6.4 %collective-permute-done.2.partner_ref = bf16[512,128]{1,0:T(8,128)(2,1)S(1)} collective-permute-done((bf16[512,128]{1,0:T(8,128)(2,1)S(1)}, bf16[512,128]{1,0:T(8,128)(2,1)S(1)}, u32[]{:S(2)}, u32[]{:S(2)}) %collective-permute-start.2) | collective-permute-done | bytes 131104 | tf_op jit(solution)/shard_map/ppermute | solution.py:13
  20.7 0.2 partner.5.coefficients_ref
  20.9 4.7 %collective-permute-start.3 = (bf16[512,128]{1,0:T(8,128)(2,1)S(1)}, bf16[512,128]{1,0:T(8,128)(2,1)S(1)}, u32[]{:S(2)}, u32[]{:S(2)}) collective-permute-start(bf16[512,128]{1,0:T(8,128)(2,1)S(1)} %partner.5.coefficients_ref), channel_id=1, source_target_pairs={{0,8},{1,9},{2,10},{3,11},{4,12},{5,13},{6,14},{7,15},{8,0},{9,1},... | collective-permute-start | bytes 393224 | tf_op jit(solution)/shard_map/ppermute | solution.py:13
  25.6 0.2 own.7.own_term_ref
  25.9 0.0 copy-start
  25.9 7.3 %collective-permute-done.3.partner_ref = bf16[512,128]{1,0:T(8,128)(2,1)S(1)} collective-permute-done((bf16[512,128]{1,0:T(8,128)(2,1)S(1)}, bf16[512,128]{1,0:T(8,128)(2,1)S(1)}, u32[]{:S(2)}, u32[]{:S(2)}) %collective-permute-start.3) | collective-permute-done | bytes 131104 | tf_op jit(solution)/shard_map/ppermute | solution.py:13
  33.1 0.5 last.1
  33.6 3.3 %collective-permute-start.5 = (bf16[512,128]{1,0:T(8,128)(2,1)S(1)}, bf16[512,128]{1,0:T(8,128)(2,1)S(1)}, u32[]{:S(2)}, u32[]{:S(2)}) collective-permute-start(bf16[512,128]{1,0:T(8,128)(2,1)S(1)} %get-tuple-element.15), channel_id=1, source_target_pairs={{0,32},{32,0},{64,96},{96,64},{128,160},{160,128},{192,224},{224,1... | collective-permute-start | bytes 393224 | tf_op jit(solution)/shard_map/ppermute | solution.py:13
  36.9 1.1 %collective-permute-start.7 = (bf16[512,128]{1,0:T(8,128)(2,1)S(1)}, bf16[512,128]{1,0:T(8,128)(2,1)S(1)}, u32[]{:S(2)}, u32[]{:S(2)}) collective-permute-start(bf16[512,128]{1,0:T(8,128)(2,1)S(1)} %get-tuple-element.16), channel_id=1, source_target_pairs={{0,48},{1,49},{2,50},{3,51},{4,52},{5,53},{6,54},{7,55},{8,56},{9,... | collective-permute-start | bytes 393224 | tf_op jit(solution)/shard_map/ppermute | solution.py:13
  38.0 0.0 collective-permute-start.6
  38.0 2.5 %collective-permute-done.5 = bf16[512,128]{1,0:T(8,128)(2,1)S(1)} collective-permute-done((bf16[512,128]{1,0:T(8,128)(2,1)S(1)}, bf16[512,128]{1,0:T(8,128)(2,1)S(1)}, u32[]{:S(2)}, u32[]{:S(2)}) %collective-permute-start.5) | collective-permute-done | bytes 131104 | tf_op jit(solution)/shard_map/ppermute | solution.py:13
  40.5 2.6 %collective-permute-done.7 = bf16[512,128]{1,0:T(8,128)(2,1)S(1)} collective-permute-done((bf16[512,128]{1,0:T(8,128)(2,1)S(1)}, bf16[512,128]{1,0:T(8,128)(2,1)S(1)}, u32[]{:S(2)}, u32[]{:S(2)}) %collective-permute-start.7) | collective-permute-done | bytes 131104 | tf_op jit(solution)/shard_map/ppermute | solution.py:13
  43.1 0.3 collective-permute-done.6
  43.4 0.1 add_convert_fusion.refs_0_
  43.5 2.8 %collective-permute-start.10 = (bf16[512,128]{1,0:T(8,128)(2,1)S(1)}, bf16[512,128]{1,0:T(8,128)(2,1)S(1)}, u32[]{:S(2)}, u32[]{:S(2)}) collective-permute-start(bf16[512,128]{1,0:T(8,128)(2,1)S(1)} %add_convert_fusion.refs_0_), channel_id=1, source_target_pairs={{0,192},{32,224},{64,128},{96,160},{128,64},{160,96},{192,0},{224,... | collective-permute-start | bytes 393224 | tf_op jit(solution)/shard_map/ppermute | solution.py:13
  46.3 0.8 %collective-permute-start.9 = (bf16[512,128]{1,0:T(8,128)(2,1)S(1)}, bf16[512,128]{1,0:T(8,128)(2,1)S(1)}, u32[]{:S(2)}, u32[]{:S(2)}) collective-permute-start(bf16[512,128]{1,0:T(8,128)(2,1)S(1)} %add_convert_fusion.refs_0_), channel_id=1, source_target_pairs={{0,128},{32,160},{64,192},{96,224},{128,0},{160,32},{192,64},{224,... | collective-permute-start | bytes 393224 | tf_op jit(solution)/shard_map/ppermute | solution.py:13
  47.1 0.6 %collective-permute-start.8 = (bf16[512,128]{1,0:T(8,128)(2,1)S(1)}, bf16[512,128]{1,0:T(8,128)(2,1)S(1)}, u32[]{:S(2)}, u32[]{:S(2)}) collective-permute-start(bf16[512,128]{1,0:T(8,128)(2,1)S(1)} %add_convert_fusion.refs_0_), channel_id=1, source_target_pairs={{0,64},{32,96},{64,0},{96,32},{128,192},{160,224},{192,128},{224,1... | collective-permute-start | bytes 393224 | tf_op jit(solution)/shard_map/ppermute | solution.py:13
  47.6 3.5 %collective-permute-done.10.refs_3_ = bf16[512,128]{1,0:T(8,128)(2,1)S(1)} collective-permute-done((bf16[512,128]{1,0:T(8,128)(2,1)S(1)}, bf16[512,128]{1,0:T(8,128)(2,1)S(1)}, u32[]{:S(2)}, u32[]{:S(2)}) %collective-permute-start.10) | collective-permute-done | bytes 131104 | tf_op jit(solution)/shard_map/ppermute | solution.py:13
  51.1 2.1 %collective-permute-done.9.refs_2_ = bf16[512,128]{1,0:T(8,128)(2,1)S(1)} collective-permute-done((bf16[512,128]{1,0:T(8,128)(2,1)S(1)}, bf16[512,128]{1,0:T(8,128)(2,1)S(1)}, u32[]{:S(2)}, u32[]{:S(2)}) %collective-permute-start.9) | collective-permute-done | bytes 131104 | tf_op jit(solution)/shard_map/ppermute | solution.py:13
  53.2 2.0 %expand.1 = bf16[2,128,3072]{2,1,0:T(8,128)(2,1)} custom-call(bf16[512,128]{1,0:T(8,128)(2,1)S(1)} %add_convert_fusion.refs_0_, bf16[512,128]{1,0:T(8,128)(2,1)S(1)} %collective-permute-done.8.refs_1_, bf16[512,128]{1,0:T(8,128)(2,1)S(1)} %collective-permute-done.9.refs_2_, bf16[512,128]{1,0:T(8,128)(2,1)S(1)} %collective-permute-done.10.refs_3_, ...), custom_call_target="tpu_custom_call" | custom-call | tf_op jit(solution)/shard_map/expand/pallas_call | solution.py:156
  (3 shorter events, 0.0 us)
Async XLA Ops:
  4.8 1.4 %collective-permute-start = (bf16[512,128]{1,0:T(8,128)(2,1)S(1)}, bf16[512,128]{1,0:T(8,128)(2,1)S(1)}, u32[]{:S(2)}, u32[]{:S(2)}) collective-permute-start(bf16[512,128]{1,0:T(8,128)(2,1)S(1)} %get-tuple-element.11.coefficients_ref), channel_id=1, source_target_pairs={{0,1},{1,0},{2,3},{3,2},{4,5},{5,4},{6,7},{7,6},{8,9},{9,8},{10,11... | collective-permute-start | bytes 393224 | tf_op jit(solution)/shard_map/ppermute | solution.py:13
  6.5 5.6 %collective-permute-start.1 = (bf16[512,128]{1,0:T(8,128)(2,1)S(1)}, bf16[512,128]{1,0:T(8,128)(2,1)S(1)}, u32[]{:S(2)}, u32[]{:S(2)}) collective-permute-start(bf16[512,128]{1,0:T(8,128)(2,1)S(1)} %partner.3.coefficients_ref), channel_id=1, source_target_pairs={{0,2},{1,3},{2,0},{3,1},{4,6},{5,7},{6,4},{7,5},{8,10},{9,11},{10,... | collective-permute-start | bytes 393224 | tf_op jit(solution)/shard_map/ppermute | solution.py:13
  12.3 8.4 %collective-permute-start.2 = (bf16[512,128]{1,0:T(8,128)(2,1)S(1)}, bf16[512,128]{1,0:T(8,128)(2,1)S(1)}, u32[]{:S(2)}, u32[]{:S(2)}) collective-permute-start(bf16[512,128]{1,0:T(8,128)(2,1)S(1)} %partner.4.coefficients_ref), channel_id=1, source_target_pairs={{0,4},{1,5},{2,6},{3,7},{4,0},{5,1},{6,2},{7,3},{8,12},{9,13},{10,... | collective-permute-start | bytes 393224 | tf_op jit(solution)/shard_map/ppermute | solution.py:13
  12.4 13.4 %collective-permute-start.4 = (bf16[2,256,256]{2,1,0:T(8,128)(2,1)S(1)}, bf16[2,256,256]{2,1,0:T(8,128)(2,1)S(1)}, u32[]{:S(2)}, u32[]{:S(2)}) collective-permute-start(bf16[2,256,256]{2,1,0:T(8,128)(2,1)S(1)} %get-tuple-element.14), channel_id=1, source_target_pairs={{0,16},{1,17},{2,18},{3,19},{4,20},{5,21},{6,22},{7,23},{8,24},{9,... | collective-permute-start | bytes 786440 | tf_op jit(solution)/shard_map/ppermute | solution.py:13
  20.9 12.2 %collective-permute-start.3 = (bf16[512,128]{1,0:T(8,128)(2,1)S(1)}, bf16[512,128]{1,0:T(8,128)(2,1)S(1)}, u32[]{:S(2)}, u32[]{:S(2)}) collective-permute-start(bf16[512,128]{1,0:T(8,128)(2,1)S(1)} %partner.5.coefficients_ref), channel_id=1, source_target_pairs={{0,8},{1,9},{2,10},{3,11},{4,12},{5,13},{6,14},{7,15},{8,0},{9,1},... | collective-permute-start | bytes 393224 | tf_op jit(solution)/shard_map/ppermute | solution.py:13
  25.9 27.4 %copy-start = (bf16[2,256,3072]{2,1,0:T(8,128)(2,1)S(1)}, bf16[2,256,3072]{2,1,0:T(8,128)(2,1)}, u32[]{:S(2)}) copy-start(bf16[2,256,3072]{2,1,0:T(8,128)(2,1)} %refs_4_.1) | copy-start | bytes 9437188
  33.6 6.9 %collective-permute-start.5 = (bf16[512,128]{1,0:T(8,128)(2,1)S(1)}, bf16[512,128]{1,0:T(8,128)(2,1)S(1)}, u32[]{:S(2)}, u32[]{:S(2)}) collective-permute-start(bf16[512,128]{1,0:T(8,128)(2,1)S(1)} %get-tuple-element.15), channel_id=1, source_target_pairs={{0,32},{32,0},{64,96},{96,64},{128,160},{160,128},{192,224},{224,1... | collective-permute-start | bytes 393224 | tf_op jit(solution)/shard_map/ppermute | solution.py:13
  36.9 6.2 %collective-permute-start.7 = (bf16[512,128]{1,0:T(8,128)(2,1)S(1)}, bf16[512,128]{1,0:T(8,128)(2,1)S(1)}, u32[]{:S(2)}, u32[]{:S(2)}) collective-permute-start(bf16[512,128]{1,0:T(8,128)(2,1)S(1)} %get-tuple-element.16), channel_id=1, source_target_pairs={{0,48},{1,49},{2,50},{3,51},{4,52},{5,53},{6,54},{7,55},{8,56},{9,... | collective-permute-start | bytes 393224 | tf_op jit(solution)/shard_map/ppermute | solution.py:13
  38.0 5.4 %collective-permute-start.6 = (bf16[512,128]{1,0:T(8,128)(2,1)S(1)}, bf16[512,128]{1,0:T(8,128)(2,1)S(1)}, u32[]{:S(2)}, u32[]{:S(2)}) collective-permute-start(bf16[512,128]{1,0:T(8,128)(2,1)S(1)} %get-tuple-element.16), channel_id=1, source_target_pairs={{0,16},{1,17},{2,18},{3,19},{4,20},{5,21},{6,22},{7,23},{8,24},{9,... | collective-permute-start | bytes 393224 | tf_op jit(solution)/shard_map/ppermute | solution.py:13
  43.5 7.7 %collective-permute-start.10 = (bf16[512,128]{1,0:T(8,128)(2,1)S(1)}, bf16[512,128]{1,0:T(8,128)(2,1)S(1)}, u32[]{:S(2)}, u32[]{:S(2)}) collective-permute-start(bf16[512,128]{1,0:T(8,128)(2,1)S(1)} %add_convert_fusion.refs_0_), channel_id=1, source_target_pairs={{0,192},{32,224},{64,128},{96,160},{128,64},{160,96},{192,0},{224,... | collective-permute-start | bytes 393224 | tf_op jit(solution)/shard_map/ppermute | solution.py:13
  46.3 6.9 %collective-permute-start.9 = (bf16[512,128]{1,0:T(8,128)(2,1)S(1)}, bf16[512,128]{1,0:T(8,128)(2,1)S(1)}, u32[]{:S(2)}, u32[]{:S(2)}) collective-permute-start(bf16[512,128]{1,0:T(8,128)(2,1)S(1)} %add_convert_fusion.refs_0_), channel_id=1, source_target_pairs={{0,128},{32,160},{64,192},{96,224},{128,0},{160,32},{192,64},{224,... | collective-permute-start | bytes 393224 | tf_op jit(solution)/shard_map/ppermute | solution.py:13
  47.1 6.2 %collective-permute-start.8 = (bf16[512,128]{1,0:T(8,128)(2,1)S(1)}, bf16[512,128]{1,0:T(8,128)(2,1)S(1)}, u32[]{:S(2)}, u32[]{:S(2)}) collective-permute-start(bf16[512,128]{1,0:T(8,128)(2,1)S(1)} %add_convert_fusion.refs_0_), channel_id=1, source_target_pairs={{0,64},{32,96},{64,0},{96,32},{128,192},{160,224},{192,128},{224,1... | collective-permute-start | bytes 393224 | tf_op jit(solution)/shard_map/ppermute | solution.py:13
